TPU v7x, 32 devices: a whole 2x2x4 slice. The times are simulated.
32 devices in a mesh: rows: 8 (over z, y), cols: 4 (over x, core).
Axes of the slice: x: 2, y: 2, z: 4, core: 2. Of those that a mesh axis runs over, the one named last changes fastest.
Arguments:
- eigenvectors: float32 [2, 4096, 1536], P(None, 'rows', 'cols'), may hold values from -6 to 6
- reflectors: float32 [8, 4, 2, 512, 256], P('rows', None, None, 'cols'), may hold values from -0.1875 to 0.1875
- tri_factors: float32 [8, 4, 2, 256, 256], P('rows', None, None, 'cols'), may hold values from -0.1875 to 0.1875
- block_order: int32 [8, 4], P('rows'), may hold values from 0 to 3, each once within a row
Outputs:
- transformed: float32 [2, 4096, 1536], P(None, 'rows', 'cols')
Inputs may be any that keep to these rules, and one draw needn't show every extreme that they name: `block_order`: each row names the stored blocks 0 to 3 once each.
All inputs are finite; a program needn't handle non-finite values.
Results may differ from a plain program's by a relative error of at most 0.00011.
Values sent between devices are 32-bit elements; how exact they have to be, the bound alone decides.
No kernel may reach another device: no remote copies, remote signals or barrier semaphores. Data moves between devices by JAX's collectives and lax.ppermute only.
A program may use at most 64 MiB of HBM per device.

v0:
```python
import functools

import jax
import jax.numpy as jnp
from jax import lax
from jax.experimental import pallas as pl
from jax.experimental.pallas import tpu as pltpu
from jax.sharding import PartitionSpec as P

LANES = 128
BF16 = jnp.bfloat16
F32 = jnp.float32


def split(x):
    hi = x.astype(BF16)
    return hi, (x - hi.astype(F32)).astype(BF16)


VMEM = pl.BlockSpec(memory_space=pltpu.VMEM)
HBM = pl.BlockSpec(memory_space=pltpu.HBM)


def limit(mib):
    return pltpu.CompilerParams(vmem_limit_bytes=mib << 20)


def pack_kernel(groups, order_hbm, v_ref, f_ref, *refs):
    outs, (order_ref, order_sem, sem) = refs[:-3], refs[-3:]
    rows = v_ref.shape[3]
    fetch = pltpu.make_async_copy(order_hbm, order_ref, order_sem)
    fetch.start()
    fetch.wait()
    copies = []
    for group, out in zip(groups, outs):
        for at, t in enumerate(group):
            k = order_ref[0, t]
            for source, part in ((v_ref, slice(0, rows)), (f_ref, slice(rows, None))):
                copies.append(
                    pltpu.make_async_copy(
                        source.at[0, k], out.at[at, :, part], sem.at[len(copies)]
                    )
                )
    for copy in copies:
        copy.start()
    for copy in copies:
        copy.wait()


def pack(order, reflectors, tri_factors, groups):
    _, _, two, v_rows, band = reflectors.shape
    shape = (two, v_rows + tri_factors.shape[3], band)
    return pl.pallas_call(
        functools.partial(pack_kernel, groups),
        in_specs=[HBM, HBM, HBM],
        out_specs=[VMEM for _ in groups],
        out_shape=[jax.ShapeDtypeStruct((len(g), *shape), F32) for g in groups],
        scratch_shapes=[
            pltpu.SMEM(order.shape, jnp.int32),
            pltpu.SemaphoreType.DMA,
            pltpu.SemaphoreType.DMA((2 * sum(map(len, groups)),)),
        ],
        compiler_params=limit(1),
        name="pack",
    )(*(pltpu.with_memory_space_constraint(x, pltpu.HBM) for x in (order, reflectors, tri_factors)))


def prep_kernel(places, v_rows, *refs):
    pieces, (vt_ref, vd_ref, ff_ref) = refs[: len(places)], refs[len(places) :]
    half = vd_ref.shape[0] // 2
    band = ff_ref.shape[0] // 2
    f_rows = pieces[0].shape[2] - v_rows
    me = lax.axis_index("cols")
    for (offset, at), piece in zip(places, pieces):
        shard = lax.bitwise_xor(me, offset)
        v_at = pl.multiple_of(shard * v_rows, v_rows)
        f_at = pl.multiple_of(shard * f_rows, f_rows)
        row = f_at + lax.broadcasted_iota(jnp.int32, (f_rows, band), 0)
        upper = lax.broadcasted_iota(jnp.int32, (f_rows, band), 1) >= row
        for part in range(2):
            lanes = slice(part * band, (part + 1) * band)
            hi, lo = split(piece[at, part, :v_rows])
            vd_ref[pl.ds(v_at, v_rows), lanes] = hi
            vd_ref[pl.ds(half + v_at, v_rows), lanes] = lo
            hi, lo = split(jnp.where(upper, piece[at, part, v_rows:], 0.0))
            ff_ref[pl.ds(f_at, f_rows), lanes] = hi
            ff_ref[pl.ds(band + f_at, f_rows), lanes] = lo
    for level in range(2):
        for part in range(2):
            block = vd_ref[level * half : (level + 1) * half, part * band : (part + 1) * band]
            vt_ref[level * band : (level + 1) * band, part * half : (part + 1) * half] = block.T


def prep(pieces, places, v_rows):
    band = pieces[0].shape[3]
    half = v_rows * len(pieces)
    shapes = [(2 * band, 2 * half), (2 * half, 2 * band), (2 * band, 2 * band)]
    return pl.pallas_call(
        functools.partial(prep_kernel, places, v_rows),
        in_specs=[VMEM for _ in pieces],
        out_specs=[VMEM for _ in shapes],
        out_shape=[jax.ShapeDtypeStruct(s, BF16) for s in shapes],
        compiler_params=limit(2),
        name="prep",
    )(*pieces)


def times(left_ref, right):
    rows = left_ref.shape[0] // 2
    hi, lo = split(right)
    both = jnp.dot(left_ref[...], hi, preferred_element_type=F32)
    return both[:rows] + both[rows:] + jnp.dot(left_ref[:rows], lo, preferred_element_type=F32)


def tick_kernel(guard_top, guard_all, chunk, *refs):
    if guard_top:
        own_ref, *refs = refs
    top_ref, low_ref, vt_ref, vd_ref, ff_ref, *refs = refs
    top_out, low_out = refs[-2:]
    section = lax.axis_index("rows")
    if chunk is not None:
        rows = top_out.shape[1]
        lanes = slice(chunk * LANES, (chunk + 1) * LANES)
        top, low = top_ref[:, :rows, lanes], low_ref[:, rows:, lanes]
    else:
        top, low = top_ref[...], low_ref[...]
    if guard_top:
        top = jnp.where(section > 0, top, own_ref[...])
    rows, lanes = top.shape[1:]
    re = jnp.concatenate([top[0], low[0]], axis=0)
    im = jnp.concatenate([top[1], low[1]], axis=0)
    w = times(
        vt_ref,
        jnp.concatenate(
            [jnp.concatenate([re, im], axis=1), jnp.concatenate([im, -re], axis=1)], axis=0
        ),
    )

    def rotate(x):
        return jnp.concatenate(
            [x, jnp.concatenate([-x[:, lanes:], x[:, :lanes]], axis=1)], axis=0
        )

    u = times(ff_ref, rotate(w))
    d = times(vd_ref, rotate(u))
    if guard_all:
        d = jnp.where(section < lax.axis_size("rows") - 1, d, 0.0)
    top_out[0] = top[0] - d[:rows, :lanes]
    top_out[1] = top[1] - d[:rows, lanes:]
    low_out[0] = low[0] - d[rows:, :lanes]
    low_out[1] = low[1] - d[rows:, lanes:]


def tick_call(factors, top, low, own=None, guard_all=False, chunk=None, rows=None):
    shape = top.shape if chunk is None else (2, rows, LANES)
    guard = own is not None
    flops = 2 * shape[2] * 2 * sum(3 * f.size // 2 for f in factors)
    return pl.pallas_call(
        functools.partial(tick_kernel, guard, guard_all, chunk),
        in_specs=[VMEM] * (5 + guard),
        out_specs=[VMEM] * 2,
        out_shape=[jax.ShapeDtypeStruct(shape, F32)] * 2,
        cost_estimate=pl.CostEstimate(
            flops=flops, transcendentals=0, bytes_accessed=sum(f.size * 2 for f in factors)
        ),
        compiler_params=limit(8),
    )(*([own] if guard else []), top, low, *factors)


def finish_kernel(chunks, first_tail, aliased, *refs):
    if aliased:
        _, *refs = refs
    *ins, out_ref, held, sem = refs
    section = lax.axis_index("rows")
    rows = out_ref.shape[1] // 2
    parts = []
    for at, tail in enumerate(ins[2 * len(chunks) :]):
        parts.append((tail, first_tail + at, rows))
    for at, c in enumerate(chunks):
        held[at] = jnp.where(section > 0, ins[at][...], ins[len(chunks) + at][...])
        parts.append((held.at[at], c, 0))
    copies = [
        pltpu.make_async_copy(
            source, out_ref.at[:, pl.ds(row, rows), pl.ds(c * LANES, LANES)], sem.at[at]
        )
        for at, (source, c, row) in enumerate(parts)
    ]
    for copy in copies:
        copy.start()
    for copy in copies:
        copy.wait()


def finish(out, shape, chunks, given, own, tails, first_tail):
    aliased = out is not None
    operands = [*([out] if aliased else []), *given, *own, *tails]
    return pl.pallas_call(
        functools.partial(finish_kernel, chunks, first_tail, aliased),
        in_specs=[HBM] * aliased + [VMEM] * (len(operands) - aliased),
        out_specs=HBM,
        out_shape=jax.ShapeDtypeStruct(shape, F32),
        scratch_shapes=[
            pltpu.VMEM((max(len(chunks), 1), *operands[-1].shape), F32),
            pltpu.SemaphoreType.DMA((len(chunks) + len(tails),)),
        ],
        input_output_aliases={0: 0} if aliased else {},
        compiler_params=limit(4),
        name="finish",
    )(*operands)


def from_behind(block, distance):
    devices = range(lax.axis_size("rows"))
    route = [(i - distance, i) for i in devices if i - distance in devices]
    return lax.ppermute(block, "rows", route)


def exchange(block, mask):
    return lax.ppermute(block, "cols", [(i, i ^ mask) for i in range(lax.axis_size("cols"))])


def shards(eigenvectors, reflectors, tri_factors, block_order):
    ticks = reflectors.shape[1]
    v_rows = reflectors.shape[3]
    band = reflectors.shape[4]
    chunks = eigenvectors.shape[2] // LANES
    members = lax.axis_size("cols")
    masks = [1 << b for b in reversed(range(members.bit_length() - 1))]

    groups = [[0], [1], list(range(2, ticks))]
    operands = (block_order, reflectors, tri_factors)
    (first,) = pack(*operands, groups[:1])
    *rest, everything = pack(*operands, groups[1:] + [list(range(ticks))])
    gathered = []
    for own in [first, *rest]:
        pieces = [(0, own)]
        for mask in masks[:-1]:
            pieces = pieces + [(o ^ mask, exchange(p, mask)) for o, p in pieces]
        gathered.append(pieces)
    partner = exchange(everything, masks[-1])

    def blocks_of(group):
        pieces = gathered[group]
        far = [(o ^ masks[-1], exchange(p, masks[-1])) for o, p in pieces[1:]]
        return pieces + far

    def factors_of(tick, blocks, at):
        places = [(o, at) for o, _ in blocks] + [(masks[-1], tick)]
        return prep([p for _, p in blocks] + [partner], places, v_rows)

    heads, tails = [None] * chunks, [None] * chunks
    given = [None] * chunks
    for tick in range(ticks):
        if tick < 3:
            blocks = blocks_of(tick)
        factors = factors_of(tick, blocks, max(tick - 2, 0))
        for c in range(chunks):
            if tick == 0:
                heads[c], tails[c] = tick_call(
                    factors, eigenvectors, eigenvectors, chunk=c, rows=band
                )
            elif tick % 2 == 0:
                heads[c], tails[c] = tick_call(factors, given[c], tails[c], own=heads[c])
            else:
                tails[c], back = tick_call(factors, tails[c], given[c], guard_all=True)
            if tick % 2 == 0:
                given[c] = from_behind(heads[c], -1)
            else:
                given[c] = from_behind(back, 1)
    shape = eigenvectors.shape
    early = list(range(chunks - 1))
    out = finish(None, shape, [], [], [], tails[:-1], 0)
    out = finish(out, shape, early, given[:-1], heads[:-1], tails[-1:], chunks - 1)
    return finish(out, shape, [chunks - 1], given[-1:], heads[-1:], [], 0)


def solution(mesh):
    return jax.shard_map(
        shards,
        mesh=mesh,
        in_specs=(
            P(None, "rows", "cols"),
            P("rows", None, None, "cols", None),
            P("rows", None, None, "cols", None),
            P("rows", None),
        ),
        out_specs=P(None, "rows", "cols"),
        check_vma=False,
    )
```

profile of v0, /device:TPU:22, one launch (start us, length us, event | category | flops | bytes accessed | tf_op | source)
XLA Modules:
  0.0 128.6 jit_solution(17586670427800019314)
XLA Ops:
  0.0 2.7 %pack.3 = (f32[1,2,192,256]{3,2,1,0:T(8,128)S(1)}, f32[2,2,192,256]{3,2,1,0:T(8,128)S(1)}, f32[4,2,192,256]{3,2,1,0:T(8,128)S(1)}) custom-call(s32[1,4]{1,0:T(1,128)} %order_hbm.3, f32[1,4,2,128,256]{4,3,2,1,0:T(8,128)} %v_ref.3, f32[1,4,2,64,256]{4,3,2,1,0:T(8,128)} %f_ref.3), custom_call_target="tpu_custom_call" | custom-call | tf_op jit(solution)/shard_map/pack/pallas_call | solution.py:53
  2.7 0.1 collective-permute-start.2
  2.8 0.6 collective-permute-start.7
  3.4 1.7 %pack.2.refs_0_ = f32[1,2,192,256]{3,2,1,0:T(8,128)S(1)} custom-call(s32[1,4]{1,0:T(1,128)} %order_hbm.3, f32[1,4,2,128,256]{4,3,2,1,0:T(8,128)} %v_ref.3, f32[1,4,2,64,256]{4,3,2,1,0:T(8,128)} %f_ref.3), custom_call_target="tpu_custom_call" | custom-call | tf_op jit(solution)/shard_map/pack/pallas_call | solution.py:53
  5.1 0.0 copy-start
  5.1 1.6 %collective-permute-start = (f32[1,2,192,256]{3,2,1,0:T(8,128)S(1)}, f32[1,2,192,256]{3,2,1,0:T(8,128)S(1)}, u32[]{:S(2)}, u32[]{:S(2)}) collective-permute-start(f32[1,2,192,256]{3,2,1,0:T(8,128)S(1)} %pack.2.refs_0_), channel_id=1, source_target_pairs={{0,2},{1,3},{2,0},{3,1},{4,6},{5,7},{6,4},{7,5},{8,10},{9,11},{10,... | collective-permute-start | bytes 1179656 | tf_op jit(solution)/shard_map/ppermute | solution.py:219
  6.7 0.5 collective-permute-start.4
  7.2 24.5 %collective-permute-done.refs_1_ = f32[1,2,192,256]{3,2,1,0:T(8,128)S(1)} collective-permute-done((f32[1,2,192,256]{3,2,1,0:T(8,128)S(1)}, f32[1,2,192,256]{3,2,1,0:T(8,128)S(1)}, u32[]{:S(2)}, u32[]{:S(2)}) %collective-permute-start) | collective-permute-done | bytes 393248 | tf_op jit(solution)/shard_map/ppermute | solution.py:219
  31.7 0.5 collective-permute-start.8
  32.2 7.4 %collective-permute-done.4.refs_1_ = f32[1,2,192,256]{3,2,1,0:T(8,128)S(1)} collective-permute-done((f32[1,2,192,256]{3,2,1,0:T(8,128)S(1)}, f32[1,2,192,256]{3,2,1,0:T(8,128)S(1)}, u32[]{:S(2)}, u32[]{:S(2)}) %collective-permute-start.4) | collective-permute-done | bytes 393248 | tf_op jit(solution)/shard_map/ppermute | solution.py:219
  39.6 0.0 collective-permute-start.5
  39.6 0.0 collective-permute-done.1.refs_2_
  39.6 0.6 prep.4
  40.2 2.2 %shard_map.50 = (f32[2,256,128]{2,1,0:T(8,128)S(1)}, f32[2,256,128]{2,1,0:T(8,128)S(1)}) custom-call(f32[2,512,384]{2,1,0:T(8,128)S(1)} %copy-done, f32[2,512,384]{2,1,0:T(8,128)S(1)} %copy-done, bf16[512,1024]{1,0:T(8,128)(2,1)S(1)} %get-tuple-element.45.refs_2_, bf16[1024,512]{1,0:T(8,128)(2,1)S(1)} %get-tuple-element.46.refs_3_, ...), custom_call_target="tpu_custom_call" | custom-call | flops 1006632960 | bytes 2621440 | tf_op jit(solution)/shard_map/pallas_call | solution.py:158
  42.4 2.5 %collective-permute-start.10 = (f32[2,256,128]{2,1,0:T(8,128)S(1)}, f32[2,256,128]{2,1,0:T(8,128)S(1)}, u32[]{:S(2)}, u32[]{:S(2)}) collective-permute-start(f32[2,256,128]{2,1,0:T(8,128)S(1)} %get-tuple-element.66.refs_0_), channel_id=1, source_target_pairs={{4,0},{8,4},{12,8},{16,12},{20,16},{24,20},{28,24},{5,1},{9,5},{13... | collective-permute-start | bytes 786440 | tf_op jit(solution)/shard_map/ppermute | solution.py:215
  44.9 2.2 %shard_map.46 = (f32[2,256,128]{2,1,0:T(8,128)S(1)}, f32[2,256,128]{2,1,0:T(8,128)S(1)}) custom-call(f32[2,512,384]{2,1,0:T(8,128)S(1)} %copy-done, f32[2,512,384]{2,1,0:T(8,128)S(1)} %copy-done, bf16[512,1024]{1,0:T(8,128)(2,1)S(1)} %get-tuple-element.45.refs_2_, bf16[1024,512]{1,0:T(8,128)(2,1)S(1)} %get-tuple-element.46.refs_3_, ...), custom_call_target="tpu_custom_call" | custom-call | flops 1006632960 | bytes 2621440 | tf_op jit(solution)/shard_map/pallas_call | solution.py:158
  47.1 3.3 %collective-permute-start.3 = (f32[2,256,128]{2,1,0:T(8,128)S(1)}, f32[2,256,128]{2,1,0:T(8,128)S(1)}, u32[]{:S(2)}, u32[]{:S(2)}) collective-permute-start(f32[2,256,128]{2,1,0:T(8,128)S(1)} %get-tuple-element.48.refs_0_), channel_id=1, source_target_pairs={{4,0},{8,4},{12,8},{16,12},{20,16},{24,20},{28,24},{5,1},{9,5},{13... | collective-permute-start | bytes 786440 | tf_op jit(solution)/shard_map/ppermute | solution.py:215
  50.4 2.2 %shard_map.54 = (f32[2,256,128]{2,1,0:T(8,128)S(1)}, f32[2,256,128]{2,1,0:T(8,128)S(1)}) custom-call(f32[2,512,384]{2,1,0:T(8,128)S(1)} %copy-done, f32[2,512,384]{2,1,0:T(8,128)S(1)} %copy-done, bf16[512,1024]{1,0:T(8,128)(2,1)S(1)} %get-tuple-element.45.refs_2_, bf16[1024,512]{1,0:T(8,128)(2,1)S(1)} %get-tuple-element.46.refs_3_, ...), custom_call_target="tpu_custom_call" | custom-call | flops 1006632960 | bytes 2621440 | tf_op jit(solution)/shard_map/pallas_call | solution.py:158
  52.7 2.4 %collective-permute-start.15 = (f32[2,256,128]{2,1,0:T(8,128)S(1)}, f32[2,256,128]{2,1,0:T(8,128)S(1)}, u32[]{:S(2)}, u32[]{:S(2)}) collective-permute-start(f32[2,256,128]{2,1,0:T(8,128)S(1)} %get-tuple-element.75.refs_0_), channel_id=1, source_target_pairs={{4,0},{8,4},{12,8},{16,12},{20,16},{24,20},{28,24},{5,1},{9,5},{13... | collective-permute-start | bytes 786440 | tf_op jit(solution)/shard_map/ppermute | solution.py:215
  55.0 0.0 collective-permute-done.5.refs_2_
  55.1 0.6 prep.5
  55.6 2.2 %shard_map.51 = (f32[2,256,128]{2,1,0:T(8,128)S(1)}, f32[2,256,128]{2,1,0:T(8,128)S(1)}) custom-call(f32[2,256,128]{2,1,0:T(8,128)S(1)} %get-tuple-element.67.refs_0_, f32[2,256,128]{2,1,0:T(8,128)S(1)} %collective-permute-done.10.refs_1_, bf16[512,1024]{1,0:T(8,128)(2,1)S(1)} %get-tuple-element.51.refs_2_, bf16[1024,512]{1,0:T(8,128)(2,1)S(1)} %get-tuple-element.52.refs_3_, ...), custom_call_target="tpu_custom_call" | custom-call | flops 1006632960 | bytes 2621440 | tf_op jit(solution)/shard_map/pallas_call | solution.py:158
  57.9 4.4 %collective-permute-start.11 = (f32[2,256,128]{2,1,0:T(8,128)S(1)}, f32[2,256,128]{2,1,0:T(8,128)S(1)}, u32[]{:S(2)}, u32[]{:S(2)}) collective-permute-start(f32[2,256,128]{2,1,0:T(8,128)S(1)} %get-tuple-element.68), channel_id=1, source_target_pairs={{0,4},{4,8},{8,12},{12,16},{16,20},{20,24},{24,28},{1,5},{5,9},{9,... | collective-permute-start | bytes 786440 | tf_op jit(solution)/shard_map/ppermute | solution.py:215
  62.2 2.2 %shard_map.47 = (f32[2,256,128]{2,1,0:T(8,128)S(1)}, f32[2,256,128]{2,1,0:T(8,128)S(1)}) custom-call(f32[2,256,128]{2,1,0:T(8,128)S(1)} %get-tuple-element.49.refs_0_, f32[2,256,128]{2,1,0:T(8,128)S(1)} %collective-permute-done.3.refs_1_, bf16[512,1024]{1,0:T(8,128)(2,1)S(1)} %get-tuple-element.51.refs_2_, bf16[1024,512]{1,0:T(8,128)(2,1)S(1)} %get-tuple-element.52.refs_3_, ...), custom_call_target="tpu_custom_call" | custom-call | flops 1006632960 | bytes 2621440 | tf_op jit(solution)/shard_map/pallas_call | solution.py:158
  64.5 2.5 %collective-permute-start.6 = (f32[2,256,128]{2,1,0:T(8,128)S(1)}, f32[2,256,128]{2,1,0:T(8,128)S(1)}, u32[]{:S(2)}, u32[]{:S(2)}) collective-permute-start(f32[2,256,128]{2,1,0:T(8,128)S(1)} %get-tuple-element.54), channel_id=1, source_target_pairs={{0,4},{4,8},{8,12},{12,16},{16,20},{20,24},{24,28},{1,5},{5,9},{9,... | collective-permute-start | bytes 786440 | tf_op jit(solution)/shard_map/ppermute | solution.py:215
  67.0 6.6 %collective-permute-done.15.refs_1_ = f32[2,256,128]{2,1,0:T(8,128)S(1)} collective-permute-done((f32[2,256,128]{2,1,0:T(8,128)S(1)}, f32[2,256,128]{2,1,0:T(8,128)S(1)}, u32[]{:S(2)}, u32[]{:S(2)}) %collective-permute-start.15) | collective-permute-done | bytes 262176 | tf_op jit(solution)/shard_map/ppermute | solution.py:215
  73.6 2.2 %shard_map.55 = (f32[2,256,128]{2,1,0:T(8,128)S(1)}, f32[2,256,128]{2,1,0:T(8,128)S(1)}) custom-call(f32[2,256,128]{2,1,0:T(8,128)S(1)} %get-tuple-element.76.refs_0_, f32[2,256,128]{2,1,0:T(8,128)S(1)} %collective-permute-done.15.refs_1_, bf16[512,1024]{1,0:T(8,128)(2,1)S(1)} %get-tuple-element.51.refs_2_, bf16[1024,512]{1,0:T(8,128)(2,1)S(1)} %get-tuple-element.52.refs_3_, ...), custom_call_target="tpu_custom_call" | custom-call | flops 1006632960 | bytes 2621440 | tf_op jit(solution)/shard_map/pallas_call | solution.py:158
  75.8 8.4 %collective-permute-start.16 = (f32[2,256,128]{2,1,0:T(8,128)S(1)}, f32[2,256,128]{2,1,0:T(8,128)S(1)}, u32[]{:S(2)}, u32[]{:S(2)}) collective-permute-start(f32[2,256,128]{2,1,0:T(8,128)S(1)} %get-tuple-element.77), channel_id=1, source_target_pairs={{0,4},{4,8},{8,12},{12,16},{16,20},{20,24},{24,28},{1,5},{5,9},{9,... | collective-permute-start | bytes 786440 | tf_op jit(solution)/shard_map/ppermute | solution.py:215
  84.3 0.0 collective-permute-done.8.refs_2_
  84.3 0.6 prep.6
  84.9 2.2 %shard_map.52 = (f32[2,256,128]{2,1,0:T(8,128)S(1)}, f32[2,256,128]{2,1,0:T(8,128)S(1)}) custom-call(f32[2,256,128]{2,1,0:T(8,128)S(1)} %get-tuple-element.66.refs_0_, f32[2,256,128]{2,1,0:T(8,128)S(1)} %collective-permute-done.11.refs_1_, f32[2,256,128]{2,1,0:T(8,128)S(1)} %get-tuple-element.69.refs_2_, bf16[512,1024]{1,0:T(8,128)(2,1)S(1)} %get-tuple-element.57.refs_3_, ...), custom_call_target="tpu_custom_call" | custom-call | flops 1006632960 | bytes 2621440 | tf_op jit(solution)/shard_map/pallas_call | solution.py:158
  87.1 2.1 %collective-permute-start.12 = (f32[2,256,128]{2,1,0:T(8,128)S(1)}, f32[2,256,128]{2,1,0:T(8,128)S(1)}, u32[]{:S(2)}, u32[]{:S(2)}) collective-permute-start(f32[2,256,128]{2,1,0:T(8,128)S(1)} %get-tuple-element.71.refs_4_), channel_id=1, source_target_pairs={{4,0},{8,4},{12,8},{16,12},{20,16},{24,20},{28,24},{5,1},{9,5},{13... | collective-permute-start | bytes 786440 | tf_op jit(solution)/shard_map/ppermute | solution.py:215
  89.2 2.2 %shard_map.48 = (f32[2,256,128]{2,1,0:T(8,128)S(1)}, f32[2,256,128]{2,1,0:T(8,128)S(1)}) custom-call(f32[2,256,128]{2,1,0:T(8,128)S(1)} %get-tuple-element.48.refs_0_, f32[2,256,128]{2,1,0:T(8,128)S(1)} %collective-permute-done.6.refs_1_, f32[2,256,128]{2,1,0:T(8,128)S(1)} %get-tuple-element.55.refs_2_, bf16[512,1024]{1,0:T(8,128)(2,1)S(1)} %get-tuple-element.57.refs_3_, ...), custom_call_target="tpu_custom_call" | custom-call | flops 1006632960 | bytes 2621440 | tf_op jit(solution)/shard_map/pallas_call | solution.py:158
  91.4 1.9 %collective-permute-start.9 = (f32[2,256,128]{2,1,0:T(8,128)S(1)}, f32[2,256,128]{2,1,0:T(8,128)S(1)}, u32[]{:S(2)}, u32[]{:S(2)}) collective-permute-start(f32[2,256,128]{2,1,0:T(8,128)S(1)} %get-tuple-element.61.refs_3_), channel_id=1, source_target_pairs={{4,0},{8,4},{12,8},{16,12},{20,16},{24,20},{28,24},{5,1},{9,5},{13... | collective-permute-start | bytes 786440 | tf_op jit(solution)/shard_map/ppermute | solution.py:215
  93.4 2.2 %shard_map.56 = (f32[2,256,128]{2,1,0:T(8,128)S(1)}, f32[2,256,128]{2,1,0:T(8,128)S(1)}) custom-call(f32[2,256,128]{2,1,0:T(8,128)S(1)} %get-tuple-element.75.refs_0_, f32[2,256,128]{2,1,0:T(8,128)S(1)} %collective-permute-done.16.refs_1_, f32[2,256,128]{2,1,0:T(8,128)S(1)} %get-tuple-element.78.refs_2_, bf16[512,1024]{1,0:T(8,128)(2,1)S(1)} %get-tuple-element.57.refs_3_, ...), custom_call_target="tpu_custom_call" | custom-call | flops 1006632960 | bytes 2621440 | tf_op jit(solution)/shard_map/pallas_call | solution.py:158
  95.6 1.9 %collective-permute-start.17 = (f32[2,256,128]{2,1,0:T(8,128)S(1)}, f32[2,256,128]{2,1,0:T(8,128)S(1)}, u32[]{:S(2)}, u32[]{:S(2)}) collective-permute-start(f32[2,256,128]{2,1,0:T(8,128)S(1)} %get-tuple-element.80.refs_2_), channel_id=1, source_target_pairs={{4,0},{8,4},{12,8},{16,12},{20,16},{24,20},{28,24},{5,1},{9,5},{13... | collective-permute-start | bytes 786440 | tf_op jit(solution)/shard_map/ppermute | solution.py:215
  97.5 0.6 prep.7
  98.1 2.2 %shard_map.53 = (f32[2,256,128]{2,1,0:T(8,128)S(1)}, f32[2,256,128]{2,1,0:T(8,128)S(1)}) custom-call(f32[2,256,128]{2,1,0:T(8,128)S(1)} %get-tuple-element.70.refs_0_, f32[2,256,128]{2,1,0:T(8,128)S(1)} %collective-permute-done.12.refs_1_, bf16[512,1024]{1,0:T(8,128)(2,1)S(1)} %get-tuple-element.62.refs_2_, bf16[1024,512]{1,0:T(8,128)(2,1)S(1)} %get-tuple-element.63.refs_3_, ...), custom_call_target="tpu_custom_call" | custom-call | flops 1006632960 | bytes 2621440 | tf_op jit(solution)/shard_map/pallas_call | solution.py:158
  100.3 4.8 %collective-permute-start.14 = (f32[2,256,128]{2,1,0:T(8,128)S(1)}, f32[2,256,128]{2,1,0:T(8,128)S(1)}, u32[]{:S(2)}, u32[]{:S(2)}) collective-permute-start(f32[2,256,128]{2,1,0:T(8,128)S(1)} %get-tuple-element.74), channel_id=1, source_target_pairs={{0,4},{4,8},{8,12},{12,16},{16,20},{20,24},{24,28},{1,5},{5,9},{9,... | collective-permute-start | bytes 786440 | tf_op jit(solution)/shard_map/ppermute | solution.py:215
  105.2 2.2 %shard_map.49 = (f32[2,256,128]{2,1,0:T(8,128)S(1)}, f32[2,256,128]{2,1,0:T(8,128)S(1)}) custom-call(f32[2,256,128]{2,1,0:T(8,128)S(1)} %get-tuple-element.60.refs_0_, f32[2,256,128]{2,1,0:T(8,128)S(1)} %collective-permute-done.9.refs_1_, bf16[512,1024]{1,0:T(8,128)(2,1)S(1)} %get-tuple-element.62.refs_2_, bf16[1024,512]{1,0:T(8,128)(2,1)S(1)} %get-tuple-element.63.refs_3_, ...), custom_call_target="tpu_custom_call" | custom-call | flops 1006632960 | bytes 2621440 | tf_op jit(solution)/shard_map/pallas_call | solution.py:158
  107.4 3.9 %collective-permute-start.13 = (f32[2,256,128]{2,1,0:T(8,128)S(1)}, f32[2,256,128]{2,1,0:T(8,128)S(1)}, u32[]{:S(2)}, u32[]{:S(2)}) collective-permute-start(f32[2,256,128]{2,1,0:T(8,128)S(1)} %get-tuple-element.73), channel_id=1, source_target_pairs={{0,4},{4,8},{8,12},{12,16},{16,20},{20,24},{24,28},{1,5},{5,9},{9,... | collective-permute-start | bytes 786440 | tf_op jit(solution)/shard_map/ppermute | solution.py:215
  111.3 2.8 %collective-permute-done.17.refs_1_ = f32[2,256,128]{2,1,0:T(8,128)S(1)} collective-permute-done((f32[2,256,128]{2,1,0:T(8,128)S(1)}, f32[2,256,128]{2,1,0:T(8,128)S(1)}, u32[]{:S(2)}, u32[]{:S(2)}) %collective-permute-start.17) | collective-permute-done | bytes 262176 | tf_op jit(solution)/shard_map/ppermute | solution.py:215
  114.1 2.2 %shard_map.57 = (f32[2,256,128]{2,1,0:T(8,128)S(1)}, f32[2,256,128]{2,1,0:T(8,128)S(1)}) custom-call(f32[2,256,128]{2,1,0:T(8,128)S(1)} %get-tuple-element.79.refs_0_, f32[2,256,128]{2,1,0:T(8,128)S(1)} %collective-permute-done.17.refs_1_, bf16[512,1024]{1,0:T(8,128)(2,1)S(1)} %get-tuple-element.62.refs_2_, bf16[1024,512]{1,0:T(8,128)(2,1)S(1)} %get-tuple-element.63.refs_3_, ...), custom_call_target="tpu_custom_call" | custom-call | flops 1006632960 | bytes 2621440 | tf_op jit(solution)/shard_map/pallas_call | solution.py:158
  116.3 7.4 %collective-permute-start.18 = (f32[2,256,128]{2,1,0:T(8,128)S(1)}, f32[2,256,128]{2,1,0:T(8,128)S(1)}, u32[]{:S(2)}, u32[]{:S(2)}) collective-permute-start(f32[2,256,128]{2,1,0:T(8,128)S(1)} %get-tuple-element.82), channel_id=1, source_target_pairs={{0,4},{4,8},{8,12},{12,16},{16,20},{20,24},{24,28},{1,5},{5,9},{9,... | collective-permute-start | bytes 786440 | tf_op jit(solution)/shard_map/ppermute | solution.py:215
  123.8 0.8 finish.3.refs_0_
  124.6 1.0 finish.4.refs_0_
  125.6 2.1 %collective-permute-done.18.refs_1_ = f32[2,256,128]{2,1,0:T(8,128)S(1)} collective-permute-done((f32[2,256,128]{2,1,0:T(8,128)S(1)}, f32[2,256,128]{2,1,0:T(8,128)S(1)}, u32[]{:S(2)}, u32[]{:S(2)}) %collective-permute-start.18) | collective-permute-done | bytes 262176 | tf_op jit(solution)/shard_map/ppermute | solution.py:215
  127.7 0.7 finish.5
  (13 shorter events, 0.0 us)
Async XLA Ops:
  2.7 36.9 %collective-permute-start.2 = (f32[4,2,192,256]{3,2,1,0:T(8,128)S(1)}, f32[4,2,192,256]{3,2,1,0:T(8,128)S(1)}, u32[]{:S(2)}, u32[]{:S(2)}) collective-permute-start(f32[4,2,192,256]{3,2,1,0:T(8,128)S(1)} %get-tuple-element.44), channel_id=1, source_target_pairs={{0,1},{1,0},{2,3},{3,2},{4,5},{5,4},{6,7},{7,6},{8,9},{9,8},{10,11... | collective-permute-start | bytes 4718600 | tf_op jit(solution)/shard_map/ppermute | solution.py:219
  2.8 28.9 %collective-permute-start.7 = (f32[2,2,192,256]{3,2,1,0:T(8,128)S(1)}, f32[2,2,192,256]{3,2,1,0:T(8,128)S(1)}, u32[]{:S(2)}, u32[]{:S(2)}) collective-permute-start(f32[2,2,192,256]{3,2,1,0:T(8,128)S(1)} %get-tuple-element.56.refs_0_), channel_id=1, source_target_pairs={{0,2},{1,3},{2,0},{3,1},{4,6},{5,7},{6,4},{7,5},{8,10},{9,11},{10,... | collective-permute-start | bytes 2359304 | tf_op jit(solution)/shard_map/ppermute | solution.py:219
  5.1 35.1 %copy-start = (f32[2,512,384]{2,1,0:T(8,128)S(1)}, f32[2,512,384]{2,1,0:T(8,128)}, u32[]{:S(2)}) copy-start(f32[2,512,384]{2,1,0:T(8,128)} %refs_1_.5) | copy-start | bytes 4718596
  5.1 26.6 %collective-permute-start = (f32[1,2,192,256]{3,2,1,0:T(8,128)S(1)}, f32[1,2,192,256]{3,2,1,0:T(8,128)S(1)}, u32[]{:S(2)}, u32[]{:S(2)}) collective-permute-start(f32[1,2,192,256]{3,2,1,0:T(8,128)S(1)} %pack.2.refs_0_), channel_id=1, source_target_pairs={{0,2},{1,3},{2,0},{3,1},{4,6},{5,7},{6,4},{7,5},{8,10},{9,11},{10,... | collective-permute-start | bytes 1179656 | tf_op jit(solution)/shard_map/ppermute | solution.py:219
  6.7 32.9 %collective-permute-start.4 = (f32[1,2,192,256]{3,2,1,0:T(8,128)S(1)}, f32[1,2,192,256]{3,2,1,0:T(8,128)S(1)}, u32[]{:S(2)}, u32[]{:S(2)}) collective-permute-start(f32[1,2,192,256]{3,2,1,0:T(8,128)S(1)} %get-tuple-element.50.refs_0_), channel_id=1, source_target_pairs={{0,2},{1,3},{2,0},{3,1},{4,6},{5,7},{6,4},{7,5},{8,10},{9,11},{10,... | collective-permute-start | bytes 1179656 | tf_op jit(solution)/shard_map/ppermute | solution.py:219
  31.7 7.9 %collective-permute-start.1 = (f32[1,2,192,256]{3,2,1,0:T(8,128)S(1)}, f32[1,2,192,256]{3,2,1,0:T(8,128)S(1)}, u32[]{:S(2)}, u32[]{:S(2)}) collective-permute-start(f32[1,2,192,256]{3,2,1,0:T(8,128)S(1)} %collective-permute-done.refs_1_), channel_id=1, source_target_pairs={{0,1},{1,0},{2,3},{3,2},{4,5},{5,4},{6,7},{7,6},{8,9},{9,8},{10,11... | collective-permute-start | bytes 1179656 | tf_op jit(solution)/shard_map/ppermute | solution.py:219
  31.7 52.5 %collective-permute-start.8 = (f32[2,2,192,256]{3,2,1,0:T(8,128)S(1)}, f32[2,2,192,256]{3,2,1,0:T(8,128)S(1)}, u32[]{:S(2)}, u32[]{:S(2)}) collective-permute-start(f32[2,2,192,256]{3,2,1,0:T(8,128)S(1)} %collective-permute-done.7.refs_1_), channel_id=1, source_target_pairs={{0,1},{1,0},{2,3},{3,2},{4,5},{5,4},{6,7},{7,6},{8,9},{9,8},{10,11... | collective-permute-start | bytes 2359304 | tf_op jit(solution)/shard_map/ppermute | solution.py:219
  39.6 15.4 %collective-permute-start.5 = (f32[1,2,192,256]{3,2,1,0:T(8,128)S(1)}, f32[1,2,192,256]{3,2,1,0:T(8,128)S(1)}, u32[]{:S(2)}, u32[]{:S(2)}) collective-permute-start(f32[1,2,192,256]{3,2,1,0:T(8,128)S(1)} %collective-permute-done.4.refs_1_), channel_id=1, source_target_pairs={{0,1},{1,0},{2,3},{3,2},{4,5},{5,4},{6,7},{7,6},{8,9},{9,8},{10,11... | collective-permute-start | bytes 1179656 | tf_op jit(solution)/shard_map/ppermute | solution.py:219
  42.4 13.2 %collective-permute-start.10 = (f32[2,256,128]{2,1,0:T(8,128)S(1)}, f32[2,256,128]{2,1,0:T(8,128)S(1)}, u32[]{:S(2)}, u32[]{:S(2)}) collective-permute-start(f32[2,256,128]{2,1,0:T(8,128)S(1)} %get-tuple-element.66.refs_0_), channel_id=1, source_target_pairs={{4,0},{8,4},{12,8},{16,12},{20,16},{24,20},{28,24},{5,1},{9,5},{13... | collective-permute-start | bytes 786440 | tf_op jit(solution)/shard_map/ppermute | solution.py:215
  47.1 15.1 %collective-permute-start.3 = (f32[2,256,128]{2,1,0:T(8,128)S(1)}, f32[2,256,128]{2,1,0:T(8,128)S(1)}, u32[]{:S(2)}, u32[]{:S(2)}) collective-permute-start(f32[2,256,128]{2,1,0:T(8,128)S(1)} %get-tuple-element.48.refs_0_), channel_id=1, source_target_pairs={{4,0},{8,4},{12,8},{16,12},{20,16},{24,20},{28,24},{5,1},{9,5},{13... | collective-permute-start | bytes 786440 | tf_op jit(solution)/shard_map/ppermute | solution.py:215
  52.7 21.0 %collective-permute-start.15 = (f32[2,256,128]{2,1,0:T(8,128)S(1)}, f32[2,256,128]{2,1,0:T(8,128)S(1)}, u32[]{:S(2)}, u32[]{:S(2)}) collective-permute-start(f32[2,256,128]{2,1,0:T(8,128)S(1)} %get-tuple-element.75.refs_0_), channel_id=1, source_target_pairs={{4,0},{8,4},{12,8},{16,12},{20,16},{24,20},{28,24},{5,1},{9,5},{13... | collective-permute-start | bytes 786440 | tf_op jit(solution)/shard_map/ppermute | solution.py:215
  57.9 27.0 %collective-permute-start.11 = (f32[2,256,128]{2,1,0:T(8,128)S(1)}, f32[2,256,128]{2,1,0:T(8,128)S(1)}, u32[]{:S(2)}, u32[]{:S(2)}) collective-permute-start(f32[2,256,128]{2,1,0:T(8,128)S(1)} %get-tuple-element.68), channel_id=1, source_target_pairs={{0,4},{4,8},{8,12},{12,16},{16,20},{20,24},{24,28},{1,5},{5,9},{9,... | collective-permute-start | bytes 786440 | tf_op jit(solution)/shard_map/ppermute | solution.py:215
  64.5 24.7 %collective-permute-start.6 = (f32[2,256,128]{2,1,0:T(8,128)S(1)}, f32[2,256,128]{2,1,0:T(8,128)S(1)}, u32[]{:S(2)}, u32[]{:S(2)}) collective-permute-start(f32[2,256,128]{2,1,0:T(8,128)S(1)} %get-tuple-element.54), channel_id=1, source_target_pairs={{0,4},{4,8},{8,12},{12,16},{16,20},{20,24},{24,28},{1,5},{5,9},{9,... | collective-permute-start | bytes 786440 | tf_op jit(solution)/shard_map/ppermute | solution.py:215
  75.8 17.5 %collective-permute-start.16 = (f32[2,256,128]{2,1,0:T(8,128)S(1)}, f32[2,256,128]{2,1,0:T(8,128)S(1)}, u32[]{:S(2)}, u32[]{:S(2)}) collective-permute-start(f32[2,256,128]{2,1,0:T(8,128)S(1)} %get-tuple-element.77), channel_id=1, source_target_pairs={{0,4},{4,8},{8,12},{12,16},{16,20},{20,24},{24,28},{1,5},{5,9},{9,... | collective-permute-start | bytes 786440 | tf_op jit(solution)/shard_map/ppermute | solution.py:215
  87.1 11.0 %collective-permute-start.12 = (f32[2,256,128]{2,1,0:T(8,128)S(1)}, f32[2,256,128]{2,1,0:T(8,128)S(1)}, u32[]{:S(2)}, u32[]{:S(2)}) collective-permute-start(f32[2,256,128]{2,1,0:T(8,128)S(1)} %get-tuple-element.71.refs_4_), channel_id=1, source_target_pairs={{4,0},{8,4},{12,8},{16,12},{20,16},{24,20},{28,24},{5,1},{9,5},{13... | collective-permute-start | bytes 786440 | tf_op jit(solution)/shard_map/ppermute | solution.py:215
  91.4 13.7 %collective-permute-start.9 = (f32[2,256,128]{2,1,0:T(8,128)S(1)}, f32[2,256,128]{2,1,0:T(8,128)S(1)}, u32[]{:S(2)}, u32[]{:S(2)}) collective-permute-start(f32[2,256,128]{2,1,0:T(8,128)S(1)} %get-tuple-element.61.refs_3_), channel_id=1, source_target_pairs={{4,0},{8,4},{12,8},{16,12},{20,16},{24,20},{28,24},{5,1},{9,5},{13... | collective-permute-start | bytes 786440 | tf_op jit(solution)/shard_map/ppermute | solution.py:215
  95.6 18.5 %collective-permute-start.17 = (f32[2,256,128]{2,1,0:T(8,128)S(1)}, f32[2,256,128]{2,1,0:T(8,128)S(1)}, u32[]{:S(2)}, u32[]{:S(2)}) collective-permute-start(f32[2,256,128]{2,1,0:T(8,128)S(1)} %get-tuple-element.80.refs_2_), channel_id=1, source_target_pairs={{4,0},{8,4},{12,8},{16,12},{20,16},{24,20},{28,24},{5,1},{9,5},{13... | collective-permute-start | bytes 786440 | tf_op jit(solution)/shard_map/ppermute | solution.py:215
  100.3 24.3 %collective-permute-start.14 = (f32[2,256,128]{2,1,0:T(8,128)S(1)}, f32[2,256,128]{2,1,0:T(8,128)S(1)}, u32[]{:S(2)}, u32[]{:S(2)}) collective-permute-start(f32[2,256,128]{2,1,0:T(8,128)S(1)} %get-tuple-element.74), channel_id=1, source_target_pairs={{0,4},{4,8},{8,12},{12,16},{16,20},{20,24},{24,28},{1,5},{5,9},{9,... | collective-permute-start | bytes 786440 | tf_op jit(solution)/shard_map/ppermute | solution.py:215
  107.4 17.2 %collective-permute-start.13 = (f32[2,256,128]{2,1,0:T(8,128)S(1)}, f32[2,256,128]{2,1,0:T(8,128)S(1)}, u32[]{:S(2)}, u32[]{:S(2)}) collective-permute-start(f32[2,256,128]{2,1,0:T(8,128)S(1)} %get-tuple-element.73), channel_id=1, source_target_pairs={{0,4},{4,8},{8,12},{12,16},{16,20},{20,24},{24,28},{1,5},{5,9},{9,... | collective-permute-start | bytes 786440 | tf_op jit(solution)/shard_map/ppermute | solution.py:215
  116.3 11.3 %collective-permute-start.18 = (f32[2,256,128]{2,1,0:T(8,128)S(1)}, f32[2,256,128]{2,1,0:T(8,128)S(1)}, u32[]{:S(2)}, u32[]{:S(2)}) collective-permute-start(f32[2,256,128]{2,1,0:T(8,128)S(1)} %get-tuple-element.82), channel_id=1, source_target_pairs={{0,4},{4,8},{8,12},{12,16},{16,20},{20,24},{24,28},{1,5},{5,9},{9,... | collective-permute-start | bytes 786440 | tf_op jit(solution)/shard_map/ppermute | solution.py:215
where the time goes:
time: 131 us; the launch traced here: 129 us
  starting transfers between devices  48.9 us (37%)
  waiting for transfers between devices  43.4 us (33%)
  Pallas kernels  35.7 us (27%)
    ppermute x12, starting transfers between devices, from_behind(): return lax.ppermute(block, 'rows', route)  45.6 us
    ppermute x7, waiting for transfers between devices, exchange(): lax.ppermute(block, 'cols', [(i, i ^ mask) for i in range(lax.axis_size('...  31.9 us
    pallas_call x12, Pallas kernels, tick_call(): pl.pallas_call(functools.partial(tick_kernel, guard, guard_all, chunk), i...  26.5 us
    ppermute x12, waiting for transfers between devices, from_behind(): return lax.ppermute(block, 'rows', route)  11.5 us
    pallas_call x2, Pallas kernels, pack(): pl.pallas_call(functools.partial(pack_kernel, groups), in_specs=[HBM, HBM...  4.39 us
    ppermute x7, starting transfers between devices, exchange(): lax.ppermute(block, 'cols', [(i, i ^ mask) for i in range(lax.axis_size('...  3.28 us
  transfers between devices with their start and end apart: 19, of which 5 were waited for; matrix products, arithmetic and copies ran while one was open for 0% of the time, Pallas kernels for 25%

commit v1 on v0

v1 whole, which is shorter than its diff:
```python
import functools

import jax
import jax.numpy as jnp
from jax import lax
from jax.experimental import pallas as pl
from jax.experimental.pallas import tpu as pltpu
from jax.sharding import PartitionSpec as P

LANES = 128
BF16 = jnp.bfloat16
F32 = jnp.float32


def split(x):
    hi = x.astype(BF16)
    return hi, (x - hi.astype(F32)).astype(BF16)


VMEM = pl.BlockSpec(memory_space=pltpu.VMEM)
HBM = pl.BlockSpec(memory_space=pltpu.HBM)


def limit(mib):
    return pltpu.CompilerParams(vmem_limit_bytes=mib << 20)


def pack_kernel(groups, order_hbm, v_ref, f_ref, *refs):
    outs, (order_ref, order_sem, sem) = refs[:-3], refs[-3:]
    rows = v_ref.shape[3]
    fetch = pltpu.make_async_copy(order_hbm, order_ref, order_sem)
    fetch.start()
    fetch.wait()
    copies = []
    for group, out in zip(groups, outs):
        for at, t in enumerate(group):
            k = order_ref[0, t]
            for source, part in ((v_ref, slice(0, rows)), (f_ref, slice(rows, None))):
                copies.append(
                    pltpu.make_async_copy(
                        source.at[0, k], out.at[at, :, part], sem.at[len(copies)]
                    )
                )
    for copy in copies:
        copy.start()
    for copy in copies:
        copy.wait()


def pack(order, reflectors, tri_factors, groups):
    _, _, two, v_rows, band = reflectors.shape
    shape = (two, v_rows + tri_factors.shape[3], band)
    return pl.pallas_call(
        functools.partial(pack_kernel, groups),
        in_specs=[HBM, HBM, HBM],
        out_specs=[VMEM for _ in groups],
        out_shape=[jax.ShapeDtypeStruct((len(g), *shape), F32) for g in groups],
        scratch_shapes=[
            pltpu.SMEM(order.shape, jnp.int32),
            pltpu.SemaphoreType.DMA,
            pltpu.SemaphoreType.DMA((2 * sum(map(len, groups)),)),
        ],
        compiler_params=limit(1),
        name="pack",
    )(*(pltpu.with_memory_space_constraint(x, pltpu.HBM) for x in (order, reflectors, tri_factors)))


def place(swapped):
    row, col = lax.axis_index("rows"), lax.axis_index("cols")
    if not swapped:
        return row, col
    low = lambda of, bit: lax.bitwise_or(of - lax.bitwise_and(of, 1), lax.bitwise_and(bit, 1))
    return low(row, col), low(col, row)


def prep_kernel(places, v_rows, swapped, *refs):
    pieces, (vt_ref, vd_ref, ff_ref) = refs[: len(places)], refs[len(places) :]
    half = vd_ref.shape[0] // 2
    band = ff_ref.shape[0] // 2
    f_rows = pieces[0].shape[2] - v_rows
    _, me = place(swapped)
    for (offset, at), piece in zip(places, pieces):
        shard = lax.bitwise_xor(me, offset)
        v_at = pl.multiple_of(shard * v_rows, v_rows)
        f_at = pl.multiple_of(shard * f_rows, f_rows)
        row = f_at + lax.broadcasted_iota(jnp.int32, (f_rows, band), 0)
        upper = lax.broadcasted_iota(jnp.int32, (f_rows, band), 1) >= row
        for part in range(2):
            lanes = slice(part * band, (part + 1) * band)
            hi, lo = split(piece[at, part, :v_rows])
            vd_ref[pl.ds(v_at, v_rows), lanes] = hi
            vd_ref[pl.ds(half + v_at, v_rows), lanes] = lo
            hi, lo = split(jnp.where(upper, piece[at, part, v_rows:], 0.0))
            ff_ref[pl.ds(f_at, f_rows), lanes] = hi
            ff_ref[pl.ds(band + f_at, f_rows), lanes] = lo
    for level in range(2):
        for part in range(2):
            block = vd_ref[level * half : (level + 1) * half, part * band : (part + 1) * band]
            vt_ref[level * band : (level + 1) * band, part * half : (part + 1) * half] = block.T


def prep(pieces, places, v_rows, swapped):
    band = pieces[0].shape[3]
    half = v_rows * len(pieces)
    shapes = [(2 * band, 2 * half), (2 * half, 2 * band), (2 * band, 2 * band)]
    return pl.pallas_call(
        functools.partial(prep_kernel, places, v_rows, swapped),
        in_specs=[VMEM for _ in pieces],
        out_specs=[VMEM for _ in shapes],
        out_shape=[jax.ShapeDtypeStruct(s, BF16) for s in shapes],
        compiler_params=limit(2),
        name="prep",
    )(*pieces)


def times(left_ref, right):
    rows = left_ref.shape[0] // 2
    hi, lo = split(right)
    both = jnp.dot(left_ref[...], hi, preferred_element_type=F32)
    return both[:rows] + both[rows:] + jnp.dot(left_ref[:rows], lo, preferred_element_type=F32)


def tick_kernel(odd, swapped, chunk, *refs):
    top_ref, low_ref, vt_ref, vd_ref, ff_ref, *refs = refs
    top_out, low_out = refs[-2:]
    if chunk is not None:
        rows = top_out.shape[1]
        lanes = slice(chunk * LANES, (chunk + 1) * LANES)
        top, low = top_ref[:, :rows, lanes], low_ref[:, rows:, lanes]
    else:
        top, low = top_ref[...], low_ref[...]
    rows, lanes = top.shape[1:]
    re = jnp.concatenate([top[0], low[0]], axis=0)
    im = jnp.concatenate([top[1], low[1]], axis=0)
    w = times(
        vt_ref,
        jnp.concatenate(
            [jnp.concatenate([re, im], axis=1), jnp.concatenate([im, -re], axis=1)], axis=0
        ),
    )

    def rotate(x):
        return jnp.concatenate(
            [x, jnp.concatenate([-x[:, lanes:], x[:, :lanes]], axis=1)], axis=0
        )

    u = times(ff_ref, rotate(w))
    d = times(vd_ref, rotate(u))
    if odd:
        section, _ = place(swapped)
        d = jnp.where(section < lax.axis_size("rows") - 1, d, 0.0)
    top_out[0] = top[0] - d[:rows, :lanes]
    top_out[1] = top[1] - d[:rows, lanes:]
    low_out[0] = low[0] - d[rows:, :lanes]
    low_out[1] = low[1] - d[rows:, lanes:]


def tick_call(factors, top, low, odd, swapped, chunk=None, rows=None):
    shape = top.shape if chunk is None else (2, rows, LANES)
    flops = 2 * shape[2] * 2 * sum(3 * f.size // 2 for f in factors)
    return pl.pallas_call(
        functools.partial(tick_kernel, odd, swapped, chunk),
        in_specs=[VMEM] * 5,
        out_specs=[VMEM] * 2,
        out_shape=[jax.ShapeDtypeStruct(shape, F32)] * 2,
        cost_estimate=pl.CostEstimate(
            flops=flops, transcendentals=0, bytes_accessed=sum(f.size * 2 for f in factors)
        ),
        compiler_params=limit(8),
    )(top, low, *factors)


def finish_kernel(parts, aliased, *refs):
    if aliased:
        _, *refs = refs
    *ins, out_ref, sem = refs
    rows = out_ref.shape[1] // 2
    copies = [
        pltpu.make_async_copy(
            source, out_ref.at[:, pl.ds(half * rows, rows), pl.ds(c * LANES, LANES)], sem.at[at]
        )
        for at, (source, (half, c)) in enumerate(zip(ins, parts))
    ]
    for copy in copies:
        copy.start()
    for copy in copies:
        copy.wait()


def finish(out, shape, blocks):
    aliased = out is not None
    operands = [*([out] if aliased else []), *(b for _, b in blocks)]
    return pl.pallas_call(
        functools.partial(finish_kernel, tuple(p for p, _ in blocks), aliased),
        in_specs=[HBM] * aliased + [VMEM] * len(blocks),
        out_specs=HBM,
        out_shape=jax.ShapeDtypeStruct(shape, F32),
        scratch_shapes=[pltpu.SemaphoreType.DMA((len(blocks),))],
        input_output_aliases={0: 0} if aliased else {},
        compiler_params=limit(4),
        name="finish",
    )(*operands)


def plain(section, block):
    return section, block


def swapped(section, block):
    return section - section % 2 + block % 2, block - block % 2 + section % 2


def move(value, source, target, step=0, flip=0):
    sections, blocks = lax.axis_size("rows"), lax.axis_size("cols")
    flat = lambda at: at[0] * blocks + at[1]
    route = [
        (flat(source(s, b)), flat(target((s + step) % sections, b ^ flip)))
        for s in range(sections)
        for b in range(blocks)
    ]
    return lax.ppermute(value, ("rows", "cols"), route)


def exchange(block, mask):
    return lax.ppermute(block, "cols", [(i, i ^ mask) for i in range(lax.axis_size("cols"))])


def shards(eigenvectors, reflectors, tri_factors, block_order):
    v_rows = reflectors.shape[3]
    band = reflectors.shape[4]
    chunks = eigenvectors.shape[2] // LANES
    members = lax.axis_size("cols")
    masks = [1 << b for b in reversed(range(members.bit_length() - 1))]

    operands = (block_order, reflectors, tri_factors)
    own = [None] * 4
    (own[0],) = pack(*operands, [[0]])
    own[2], own[3] = pack(*operands, [[2], [3]])
    own[1], both = pack(*operands, [[1], [0, 1]])
    partner = exchange(both, masks[-1])
    factors = []
    for tick in range(4):
        pieces = [(0, own[tick])]
        if tick >= 2:
            pieces = [(f, move(own[tick], plain, swapped, flip=f)) for f in (0, masks[-1])]
        for mask in masks[:-1]:
            pieces = pieces + [(o ^ mask, exchange(p, mask)) for o, p in pieces]
        if tick < 2:
            pieces += [(o ^ masks[-1], exchange(p, masks[-1])) for o, p in pieces[1:]]
        places = [(o, 0) for o, _ in pieces]
        pieces = [p for _, p in pieces]
        if tick < 2:
            places, pieces = places + [(masks[-1], tick)], pieces + [partner]
        factors.append(prep(pieces, places, v_rows, tick >= 2))

    blocks = []
    for c in range(chunks):
        head, tail = tick_call(
            factors[0], eigenvectors, eigenvectors, False, False, chunk=c, rows=band
        )
        head = move(head, plain, plain, -1)
        tail, head = tick_call(factors[1], tail, head, True, False)
        tail = move(tail, plain, swapped)
        head = move(head, plain, swapped, 1)
        head, tail = tick_call(factors[2], head, tail, False, True)
        head = move(head, swapped, swapped, -1)
        tail, head = tick_call(factors[3], tail, head, True, True)
        tail = move(tail, swapped, plain)
        head = move(head, swapped, plain, 1)
        blocks.append([((1, c), tail), ((0, c), head)])
    out = finish(None, eigenvectors.shape, sum(blocks[:-1], []))
    return finish(out, eigenvectors.shape, blocks[-1])


def solution(mesh):
    return jax.shard_map(
        shards,
        mesh=mesh,
        in_specs=(
            P(None, "rows", "cols"),
            P("rows", None, None, "cols", None),
            P("rows", None, None, "cols", None),
            P("rows", None),
        ),
        out_specs=P(None, "rows", "cols"),
        check_vma=False,
    )
```

time: 131 us -> 113 us (0.86)
  the two profiles are of different devices: /device:TPU:22 before, /device:TPU:1 now
where the time goes in v1:
time: 113 us
  starting transfers between devices  55.5 us (49%)
  Pallas kernels  36 us (32%)
  waiting for transfers between devices  20.8 us (18%)
    ppermute x22, starting transfers between devices, move(): return lax.ppermute(value, ('rows', 'cols'), route)  45.7 us
    pallas_call x12, Pallas kernels, tick_call(): pl.pallas_call(functools.partial(tick_kernel, odd, swapped, chunk), in_sp...  26.5 us
    ppermute x22, waiting for transfers between devices, move(): return lax.ppermute(value, ('rows', 'cols'), route)  14.6 us
    ppermute x9, starting transfers between devices, exchange(): lax.ppermute(block, 'cols', [(i, i ^ mask) for i in range(lax.axis_size('...  9.83 us
    ppermute x9, waiting for transfers between devices, exchange(): lax.ppermute(block, 'cols', [(i, i ^ mask) for i in range(lax.axis_size('...  6.24 us
    pallas_call x3, Pallas kernels, pack(): pl.pallas_call(functools.partial(pack_kernel, groups), in_specs=[HBM, HBM...  5.47 us
  transfers between devices with their start and end apart: 31, of which 6 were waited for; matrix products, arithmetic and copies ran while one was open for 0% of the time, Pallas kernels for 30%

profile of v1, /device:TPU:1, one launch (start us, length us, event | category | flops | bytes accessed | tf_op | source)
XLA Modules:
  0.0 112.9 jit_solution(12400672978791112606)
XLA Ops:
  0.0 1.7 %pack.3.refs_0_ = f32[1,2,192,256]{3,2,1,0:T(8,128)S(1)} custom-call(s32[1,4]{1,0:T(1,128)} %order_hbm.5, f32[1,4,2,128,256]{4,3,2,1,0:T(8,128)} %v_ref.5, f32[1,4,2,64,256]{4,3,2,1,0:T(8,128)} %f_ref.5), custom_call_target="tpu_custom_call" | custom-call | tf_op jit(solution)/shard_map/pack/pallas_call | solution.py:53
  1.7 2.1 %collective-permute-start = (f32[1,2,192,256]{3,2,1,0:T(8,128)S(1)}, f32[1,2,192,256]{3,2,1,0:T(8,128)S(1)}, u32[]{:S(2)}, u32[]{:S(2)}) collective-permute-start(f32[1,2,192,256]{3,2,1,0:T(8,128)S(1)} %pack.3.refs_0_), channel_id=1, source_target_pairs={{0,2},{1,3},{2,0},{3,1},{4,6},{5,7},{6,4},{7,5},{8,10},{9,11},{10,... | collective-permute-start | bytes 1179656 | tf_op jit(solution)/shard_map/ppermute | solution.py:225
  3.8 2.0 %pack.4 = (f32[1,2,192,256]{3,2,1,0:T(8,128)S(1)}, f32[2,2,192,256]{3,2,1,0:T(8,128)S(1)}) custom-call(s32[1,4]{1,0:T(1,128)} %order_hbm.5, f32[1,4,2,128,256]{4,3,2,1,0:T(8,128)} %v_ref.5, f32[1,4,2,64,256]{4,3,2,1,0:T(8,128)} %f_ref.5), custom_call_target="tpu_custom_call" | custom-call | tf_op jit(solution)/shard_map/pack/pallas_call | solution.py:53
  5.8 1.0 collective-permute-start.2
  6.8 5.8 %collective-permute-done.refs_1_ = f32[1,2,192,256]{3,2,1,0:T(8,128)S(1)} collective-permute-done((f32[1,2,192,256]{3,2,1,0:T(8,128)S(1)}, f32[1,2,192,256]{3,2,1,0:T(8,128)S(1)}, u32[]{:S(2)}, u32[]{:S(2)}) %collective-permute-start) | collective-permute-done | bytes 393248 | tf_op jit(solution)/shard_map/ppermute | solution.py:225
  12.6 2.1 %collective-permute-start.1 = (f32[1,2,192,256]{3,2,1,0:T(8,128)S(1)}, f32[1,2,192,256]{3,2,1,0:T(8,128)S(1)}, u32[]{:S(2)}, u32[]{:S(2)}) collective-permute-start(f32[1,2,192,256]{3,2,1,0:T(8,128)S(1)} %collective-permute-done.refs_1_), channel_id=1, source_target_pairs={{0,1},{1,0},{2,3},{3,2},{4,5},{5,4},{6,7},{7,6},{8,9},{9,8},{10,11... | collective-permute-start | bytes 1179656 | tf_op jit(solution)/shard_map/ppermute | solution.py:225
  14.7 1.8 %pack.5 = (f32[1,2,192,256]{3,2,1,0:T(8,128)S(1)}, f32[1,2,192,256]{3,2,1,0:T(8,128)S(1)}) custom-call(s32[1,4]{1,0:T(1,128)} %order_hbm.5, f32[1,4,2,128,256]{4,3,2,1,0:T(8,128)} %v_ref.5, f32[1,4,2,64,256]{4,3,2,1,0:T(8,128)} %f_ref.5), custom_call_target="tpu_custom_call" | custom-call | tf_op jit(solution)/shard_map/pack/pallas_call | solution.py:53
  16.6 4.0 %collective-permute-start.8 = (f32[1,2,192,256]{3,2,1,0:T(8,128)S(1)}, f32[1,2,192,256]{3,2,1,0:T(8,128)S(1)}, u32[]{:S(2)}, u32[]{:S(2)}) collective-permute-start(f32[1,2,192,256]{3,2,1,0:T(8,128)S(1)} %get-tuple-element.57), channel_id=1, source_target_pairs={{0,0},{1,4},{2,2},{3,6},{4,1},{5,5},{6,3},{7,7},{8,8},{9,12},{10,1... | collective-permute-start | bytes 1179656 | tf_op jit(solution)/shard_map/ppermute | solution.py:221
  20.6 0.4 collective-permute-done.4.refs_1_
  21.0 1.3 %collective-permute-start.5 = (f32[1,2,192,256]{3,2,1,0:T(8,128)S(1)}, f32[1,2,192,256]{3,2,1,0:T(8,128)S(1)}, u32[]{:S(2)}, u32[]{:S(2)}) collective-permute-start(f32[1,2,192,256]{3,2,1,0:T(8,128)S(1)} %collective-permute-done.4.refs_1_), channel_id=1, source_target_pairs={{0,1},{1,0},{2,3},{3,2},{4,5},{5,4},{6,7},{7,6},{8,9},{9,8},{10,11... | collective-permute-start | bytes 1179656 | tf_op jit(solution)/shard_map/ppermute | solution.py:225
  22.3 0.6 prep.4
  22.9 2.2 %shard_map.54 = (f32[2,256,128]{2,1,0:T(8,128)S(1)}, f32[2,256,128]{2,1,0:T(8,128)S(1)}) custom-call(f32[2,512,384]{2,1,0:T(8,128)S(1)} %copy-done, f32[2,512,384]{2,1,0:T(8,128)S(1)} %copy-done, bf16[512,1024]{1,0:T(8,128)(2,1)S(1)} %get-tuple-element.46.refs_2_, bf16[1024,512]{1,0:T(8,128)(2,1)S(1)} %get-tuple-element.47.refs_3_, ...), custom_call_target="tpu_custom_call" | custom-call | flops 1006632960 | bytes 2621440 | tf_op jit(solution)/shard_map/pallas_call | solution.py:161
  25.1 4.6 %collective-permute-start.25 = (f32[2,256,128]{2,1,0:T(8,128)S(1)}, f32[2,256,128]{2,1,0:T(8,128)S(1)}, u32[]{:S(2)}, u32[]{:S(2)}) collective-permute-start(f32[2,256,128]{2,1,0:T(8,128)S(1)} %get-tuple-element.78), channel_id=1, source_target_pairs={{0,28},{1,29},{2,30},{3,31},{4,0},{5,1},{6,2},{7,3},{8,4},{9,5},{1... | collective-permute-start | bytes 786440 | tf_op jit(solution)/shard_map/ppermute | solution.py:221
  29.7 0.3 collective-permute-start.14
  29.9 2.2 %shard_map.50 = (f32[2,256,128]{2,1,0:T(8,128)S(1)}, f32[2,256,128]{2,1,0:T(8,128)S(1)}) custom-call(f32[2,512,384]{2,1,0:T(8,128)S(1)} %copy-done, f32[2,512,384]{2,1,0:T(8,128)S(1)} %copy-done, bf16[512,1024]{1,0:T(8,128)(2,1)S(1)} %get-tuple-element.46.refs_2_, bf16[1024,512]{1,0:T(8,128)(2,1)S(1)} %get-tuple-element.47.refs_3_, ...), custom_call_target="tpu_custom_call" | custom-call | flops 1006632960 | bytes 2621440 | tf_op jit(solution)/shard_map/pallas_call | solution.py:161
  32.2 1.9 %collective-permute-start.13 = (f32[1,2,192,256]{3,2,1,0:T(8,128)S(1)}, f32[1,2,192,256]{3,2,1,0:T(8,128)S(1)}, u32[]{:S(2)}, u32[]{:S(2)}) collective-permute-start(f32[1,2,192,256]{3,2,1,0:T(8,128)S(1)} %get-tuple-element.63), channel_id=1, source_target_pairs={{0,0},{1,4},{2,2},{3,6},{4,1},{5,5},{6,3},{7,7},{8,8},{9,12},{10,1... | collective-permute-start | bytes 1179656 | tf_op jit(solution)/shard_map/ppermute | solution.py:221
  34.1 1.3 %collective-permute-start.11 = (f32[1,2,192,256]{3,2,1,0:T(8,128)S(1)}, f32[1,2,192,256]{3,2,1,0:T(8,128)S(1)}, u32[]{:S(2)}, u32[]{:S(2)}) collective-permute-start(f32[1,2,192,256]{3,2,1,0:T(8,128)S(1)} %collective-permute-done.9.refs_1_), channel_id=1, source_target_pairs={{0,2},{1,3},{2,0},{3,1},{4,6},{5,7},{6,4},{7,5},{8,10},{9,11},{10,... | collective-permute-start | bytes 1179656 | tf_op jit(solution)/shard_map/ppermute | solution.py:225
  35.4 0.6 prep.5
  36.0 0.6 collective-permute-start.10
  36.5 2.2 %shard_map.46 = (f32[2,256,128]{2,1,0:T(8,128)S(1)}, f32[2,256,128]{2,1,0:T(8,128)S(1)}) custom-call(f32[2,512,384]{2,1,0:T(8,128)S(1)} %copy-done, f32[2,512,384]{2,1,0:T(8,128)S(1)} %copy-done, bf16[512,1024]{1,0:T(8,128)(2,1)S(1)} %get-tuple-element.46.refs_2_, bf16[1024,512]{1,0:T(8,128)(2,1)S(1)} %get-tuple-element.47.refs_3_, ...), custom_call_target="tpu_custom_call" | custom-call | flops 1006632960 | bytes 2621440 | tf_op jit(solution)/shard_map/pallas_call | solution.py:161
  38.7 2.2 %shard_map.55 = (f32[2,256,128]{2,1,0:T(8,128)S(1)}, f32[2,256,128]{2,1,0:T(8,128)S(1)}) custom-call(f32[2,256,128]{2,1,0:T(8,128)S(1)} %get-tuple-element.77.refs_0_, f32[2,256,128]{2,1,0:T(8,128)S(1)} %collective-permute-done.25.refs_1_, bf16[512,1024]{1,0:T(8,128)(2,1)S(1)} %get-tuple-element.52.refs_2_, bf16[1024,512]{1,0:T(8,128)(2,1)S(1)} %get-tuple-element.53.refs_3_, ...), custom_call_target="tpu_custom_call" | custom-call | flops 1006632960 | bytes 2621440 | tf_op jit(solution)/shard_map/pallas_call | solution.py:161
  41.0 5.0 %collective-permute-start.3 = (f32[2,256,128]{2,1,0:T(8,128)S(1)}, f32[2,256,128]{2,1,0:T(8,128)S(1)}, u32[]{:S(2)}, u32[]{:S(2)}) collective-permute-start(f32[2,256,128]{2,1,0:T(8,128)S(1)} %get-tuple-element.50), channel_id=1, source_target_pairs={{0,28},{1,29},{2,30},{3,31},{4,0},{5,1},{6,2},{7,3},{8,4},{9,5},{1... | collective-permute-start | bytes 786440 | tf_op jit(solution)/shard_map/ppermute | solution.py:221
  45.9 2.2 %shard_map.51 = (f32[2,256,128]{2,1,0:T(8,128)S(1)}, f32[2,256,128]{2,1,0:T(8,128)S(1)}) custom-call(f32[2,256,128]{2,1,0:T(8,128)S(1)} %get-tuple-element.69.refs_0_, f32[2,256,128]{2,1,0:T(8,128)S(1)} %collective-permute-done.19.refs_1_, bf16[512,1024]{1,0:T(8,128)(2,1)S(1)} %get-tuple-element.52.refs_2_, bf16[1024,512]{1,0:T(8,128)(2,1)S(1)} %get-tuple-element.53.refs_3_, ...), custom_call_target="tpu_custom_call" | custom-call | flops 1006632960 | bytes 2621440 | tf_op jit(solution)/shard_map/pallas_call | solution.py:161
  48.1 2.4 %collective-permute-done.13.refs_0_ = f32[1,2,192,256]{3,2,1,0:T(8,128)S(1)} collective-permute-done((f32[1,2,192,256]{3,2,1,0:T(8,128)S(1)}, f32[1,2,192,256]{3,2,1,0:T(8,128)S(1)}, u32[]{:S(2)}, u32[]{:S(2)}) %collective-permute-start.13) | collective-permute-done | bytes 393248 | tf_op jit(solution)/shard_map/ppermute | solution.py:221
  50.5 6.0 %collective-permute-start.20 = (f32[2,256,128]{2,1,0:T(8,128)S(1)}, f32[2,256,128]{2,1,0:T(8,128)S(1)}, u32[]{:S(2)}, u32[]{:S(2)}) collective-permute-start(f32[2,256,128]{2,1,0:T(8,128)S(1)} %get-tuple-element.71), channel_id=1, source_target_pairs={{0,1},{1,5},{2,3},{3,7},{4,8},{5,12},{6,10},{7,14},{8,9},{9,13},{1... | collective-permute-start | bytes 786440 | tf_op jit(solution)/shard_map/ppermute | solution.py:221
  56.5 2.7 %collective-permute-start.21 = (f32[2,256,128]{2,1,0:T(8,128)S(1)}, f32[2,256,128]{2,1,0:T(8,128)S(1)}, u32[]{:S(2)}, u32[]{:S(2)}) collective-permute-start(f32[2,256,128]{2,1,0:T(8,128)S(1)} %get-tuple-element.72), channel_id=1, source_target_pairs={{0,0},{1,4},{2,2},{3,6},{4,1},{5,5},{6,3},{7,7},{8,8},{9,12},{10,1... | collective-permute-start | bytes 786440 | tf_op jit(solution)/shard_map/ppermute | solution.py:221
  59.2 2.8 %collective-permute-start.27 = (f32[2,256,128]{2,1,0:T(8,128)S(1)}, f32[2,256,128]{2,1,0:T(8,128)S(1)}, u32[]{:S(2)}, u32[]{:S(2)}) collective-permute-start(f32[2,256,128]{2,1,0:T(8,128)S(1)} %get-tuple-element.80), channel_id=1, source_target_pairs={{0,0},{1,4},{2,2},{3,6},{4,1},{5,5},{6,3},{7,7},{8,8},{9,12},{10,1... | collective-permute-start | bytes 786440 | tf_op jit(solution)/shard_map/ppermute | solution.py:221
  62.1 1.3 %collective-permute-start.16 = (f32[1,2,192,256]{3,2,1,0:T(8,128)S(1)}, f32[1,2,192,256]{3,2,1,0:T(8,128)S(1)}, u32[]{:S(2)}, u32[]{:S(2)}) collective-permute-start(f32[1,2,192,256]{3,2,1,0:T(8,128)S(1)} %collective-permute-done.14.refs_1_), channel_id=1, source_target_pairs={{0,2},{1,3},{2,0},{3,1},{4,6},{5,7},{6,4},{7,5},{8,10},{9,11},{10,... | collective-permute-start | bytes 1179656 | tf_op jit(solution)/shard_map/ppermute | solution.py:225
  63.6 0.6 prep.6
  64.2 2.2 %shard_map.47 = (f32[2,256,128]{2,1,0:T(8,128)S(1)}, f32[2,256,128]{2,1,0:T(8,128)S(1)}) custom-call(f32[2,256,128]{2,1,0:T(8,128)S(1)} %get-tuple-element.49.refs_0_, f32[2,256,128]{2,1,0:T(8,128)S(1)} %collective-permute-done.3.refs_1_, bf16[512,1024]{1,0:T(8,128)(2,1)S(1)} %get-tuple-element.52.refs_2_, bf16[1024,512]{1,0:T(8,128)(2,1)S(1)} %get-tuple-element.53.refs_3_, ...), custom_call_target="tpu_custom_call" | custom-call | flops 1006632960 | bytes 2621440 | tf_op jit(solution)/shard_map/pallas_call | solution.py:161
  66.5 0.7 collective-permute-done.21.refs_1_
  67.2 4.6 %collective-permute-start.7 = (f32[2,256,128]{2,1,0:T(8,128)S(1)}, f32[2,256,128]{2,1,0:T(8,128)S(1)}, u32[]{:S(2)}, u32[]{:S(2)}) collective-permute-start(f32[2,256,128]{2,1,0:T(8,128)S(1)} %get-tuple-element.56), channel_id=1, source_target_pairs={{0,0},{1,4},{2,2},{3,6},{4,1},{5,5},{6,3},{7,7},{8,8},{9,12},{10,1... | collective-permute-start | bytes 786440 | tf_op jit(solution)/shard_map/ppermute | solution.py:221
  71.8 2.2 %shard_map.52 = (f32[2,256,128]{2,1,0:T(8,128)S(1)}, f32[2,256,128]{2,1,0:T(8,128)S(1)}) custom-call(f32[2,256,128]{2,1,0:T(8,128)S(1)} %collective-permute-done.20.refs_0_, f32[2,256,128]{2,1,0:T(8,128)S(1)} %collective-permute-done.21.refs_1_, bf16[512,1024]{1,0:T(8,128)(2,1)S(1)} %get-tuple-element.58.refs_2_, ...), custom_call_target="tpu_custom_call" | custom-call | flops 1006632960 | bytes 2621440 | tf_op jit(solution)/shard_map/pallas_call | solution.py:161
  74.1 2.2 %shard_map.56 = (f32[2,256,128]{2,1,0:T(8,128)S(1)}, f32[2,256,128]{2,1,0:T(8,128)S(1)}) custom-call(f32[2,256,128]{2,1,0:T(8,128)S(1)} %collective-permute-done.26.refs_0_, f32[2,256,128]{2,1,0:T(8,128)S(1)} %collective-permute-done.27.refs_1_, bf16[512,1024]{1,0:T(8,128)(2,1)S(1)} %get-tuple-element.58.refs_2_, ...), custom_call_target="tpu_custom_call" | custom-call | flops 1006632960 | bytes 2621440 | tf_op jit(solution)/shard_map/pallas_call | solution.py:161
  76.3 5.3 %collective-permute-start.28 = (f32[2,256,128]{2,1,0:T(8,128)S(1)}, f32[2,256,128]{2,1,0:T(8,128)S(1)}, u32[]{:S(2)}, u32[]{:S(2)}) collective-permute-start(f32[2,256,128]{2,1,0:T(8,128)S(1)} %get-tuple-element.82), channel_id=1, source_target_pairs={{0,25},{4,29},{2,27},{6,31},{1,0},{5,4},{3,2},{7,6},{8,1},{12,5},{... | collective-permute-start | bytes 786440 | tf_op jit(solution)/shard_map/ppermute | solution.py:221
  81.6 0.6 prep.7
  82.2 2.2 %shard_map.48 = (f32[2,256,128]{2,1,0:T(8,128)S(1)}, f32[2,256,128]{2,1,0:T(8,128)S(1)}) custom-call(f32[2,256,128]{2,1,0:T(8,128)S(1)} %collective-permute-done.6.refs_0_, f32[2,256,128]{2,1,0:T(8,128)S(1)} %collective-permute-done.7.refs_1_, bf16[512,1024]{1,0:T(8,128)(2,1)S(1)} %get-tuple-element.58.refs_2_, ...), custom_call_target="tpu_custom_call" | custom-call | flops 1006632960 | bytes 2621440 | tf_op jit(solution)/shard_map/pallas_call | solution.py:161
  84.5 2.2 %shard_map.53 = (f32[2,256,128]{2,1,0:T(8,128)S(1)}, f32[2,256,128]{2,1,0:T(8,128)S(1)}) custom-call(f32[2,256,128]{2,1,0:T(8,128)S(1)} %get-tuple-element.73.refs_0_, f32[2,256,128]{2,1,0:T(8,128)S(1)} %collective-permute-done.22.refs_1_, bf16[512,1024]{1,0:T(8,128)(2,1)S(1)} %get-tuple-element.64.refs_2_, bf16[1024,512]{1,0:T(8,128)(2,1)S(1)} %get-tuple-element.65.refs_3_, ...), custom_call_target="tpu_custom_call" | custom-call | flops 1006632960 | bytes 2621440 | tf_op jit(solution)/shard_map/pallas_call | solution.py:161
  86.7 1.9 %collective-permute-start.23 = (f32[2,256,128]{2,1,0:T(8,128)S(1)}, f32[2,256,128]{2,1,0:T(8,128)S(1)}, u32[]{:S(2)}, u32[]{:S(2)}) collective-permute-start(f32[2,256,128]{2,1,0:T(8,128)S(1)} %get-tuple-element.75), channel_id=1, source_target_pairs={{0,0},{4,1},{2,2},{6,3},{1,4},{5,5},{3,6},{7,7},{8,8},{12,9},{10,1... | collective-permute-start | bytes 786440 | tf_op jit(solution)/shard_map/ppermute | solution.py:221
  88.6 2.2 %shard_map.57 = (f32[2,256,128]{2,1,0:T(8,128)S(1)}, f32[2,256,128]{2,1,0:T(8,128)S(1)}) custom-call(f32[2,256,128]{2,1,0:T(8,128)S(1)} %get-tuple-element.81.refs_0_, f32[2,256,128]{2,1,0:T(8,128)S(1)} %collective-permute-done.28.refs_1_, bf16[512,1024]{1,0:T(8,128)(2,1)S(1)} %get-tuple-element.64.refs_2_, bf16[1024,512]{1,0:T(8,128)(2,1)S(1)} %get-tuple-element.65.refs_3_, ...), custom_call_target="tpu_custom_call" | custom-call | flops 1006632960 | bytes 2621440 | tf_op jit(solution)/shard_map/pallas_call | solution.py:161
  90.8 3.6 %collective-permute-start.29 = (f32[2,256,128]{2,1,0:T(8,128)S(1)}, f32[2,256,128]{2,1,0:T(8,128)S(1)}, u32[]{:S(2)}, u32[]{:S(2)}) collective-permute-start(f32[2,256,128]{2,1,0:T(8,128)S(1)} %get-tuple-element.83), channel_id=1, source_target_pairs={{0,0},{4,1},{2,2},{6,3},{1,4},{5,5},{3,6},{7,7},{8,8},{12,9},{10,1... | collective-permute-start | bytes 786440 | tf_op jit(solution)/shard_map/ppermute | solution.py:221
  94.6 2.2 %shard_map.49 = (f32[2,256,128]{2,1,0:T(8,128)S(1)}, f32[2,256,128]{2,1,0:T(8,128)S(1)}) custom-call(f32[2,256,128]{2,1,0:T(8,128)S(1)} %get-tuple-element.61.refs_0_, f32[2,256,128]{2,1,0:T(8,128)S(1)} %collective-permute-done.12.refs_1_, bf16[512,1024]{1,0:T(8,128)(2,1)S(1)} %get-tuple-element.64.refs_2_, bf16[1024,512]{1,0:T(8,128)(2,1)S(1)} %get-tuple-element.65.refs_3_, ...), custom_call_target="tpu_custom_call" | custom-call | flops 1006632960 | bytes 2621440 | tf_op jit(solution)/shard_map/pallas_call | solution.py:161
  96.8 1.9 %collective-permute-start.17 = (f32[2,256,128]{2,1,0:T(8,128)S(1)}, f32[2,256,128]{2,1,0:T(8,128)S(1)}, u32[]{:S(2)}, u32[]{:S(2)}) collective-permute-start(f32[2,256,128]{2,1,0:T(8,128)S(1)} %get-tuple-element.67), channel_id=1, source_target_pairs={{0,0},{4,1},{2,2},{6,3},{1,4},{5,5},{3,6},{7,7},{8,8},{12,9},{10,1... | collective-permute-start | bytes 786440 | tf_op jit(solution)/shard_map/ppermute | solution.py:221
  98.8 0.6 collective-permute-start.30
  99.5 3.1 %collective-permute-done.24.refs_3_ = f32[2,256,128]{2,1,0:T(8,128)S(1)} collective-permute-done((f32[2,256,128]{2,1,0:T(8,128)S(1)}, f32[2,256,128]{2,1,0:T(8,128)S(1)}, u32[]{:S(2)}, u32[]{:S(2)}) %collective-permute-start.24) | collective-permute-done | bytes 262176 | tf_op jit(solution)/shard_map/ppermute | solution.py:221
  102.6 8.3 %collective-permute-done.17.refs_0_ = f32[2,256,128]{2,1,0:T(8,128)S(1)} collective-permute-done((f32[2,256,128]{2,1,0:T(8,128)S(1)}, f32[2,256,128]{2,1,0:T(8,128)S(1)}, u32[]{:S(2)}, u32[]{:S(2)}) %collective-permute-start.17) | collective-permute-done | bytes 262176 | tf_op jit(solution)/shard_map/ppermute | solution.py:221
  110.9 1.0 finish.2.refs_0_
  111.9 0.8 finish.3
  (37 shorter events, 0.7 us)
Async XLA Ops:
  1.7 10.9 %collective-permute-start = (f32[1,2,192,256]{3,2,1,0:T(8,128)S(1)}, f32[1,2,192,256]{3,2,1,0:T(8,128)S(1)}, u32[]{:S(2)}, u32[]{:S(2)}) collective-permute-start(f32[1,2,192,256]{3,2,1,0:T(8,128)S(1)} %pack.3.refs_0_), channel_id=1, source_target_pairs={{0,2},{1,3},{2,0},{3,1},{4,6},{5,7},{6,4},{7,5},{8,10},{9,11},{10,... | collective-permute-start | bytes 1179656 | tf_op jit(solution)/shard_map/ppermute | solution.py:225
  5.8 16.5 %collective-permute-start.2 = (f32[2,2,192,256]{3,2,1,0:T(8,128)S(1)}, f32[2,2,192,256]{3,2,1,0:T(8,128)S(1)}, u32[]{:S(2)}, u32[]{:S(2)}) collective-permute-start(f32[2,2,192,256]{3,2,1,0:T(8,128)S(1)} %get-tuple-element.45), channel_id=1, source_target_pairs={{0,1},{1,0},{2,3},{3,2},{4,5},{5,4},{6,7},{7,6},{8,9},{9,8},{10,11... | collective-permute-start | bytes 2359304 | tf_op jit(solution)/shard_map/ppermute | solution.py:225
  6.8 16.1 %copy-start = (f32[2,512,384]{2,1,0:T(8,128)S(1)}, f32[2,512,384]{2,1,0:T(8,128)}, u32[]{:S(2)}) copy-start(f32[2,512,384]{2,1,0:T(8,128)} %refs_1_.5) | copy-start | bytes 4718596
  6.8 14.2 %collective-permute-start.4 = (f32[1,2,192,256]{3,2,1,0:T(8,128)S(1)}, f32[1,2,192,256]{3,2,1,0:T(8,128)S(1)}, u32[]{:S(2)}, u32[]{:S(2)}) collective-permute-start(f32[1,2,192,256]{3,2,1,0:T(8,128)S(1)} %get-tuple-element.51.refs_0_), channel_id=1, source_target_pairs={{0,2},{1,3},{2,0},{3,1},{4,6},{5,7},{6,4},{7,5},{8,10},{9,11},{10,... | collective-permute-start | bytes 1179656 | tf_op jit(solution)/shard_map/ppermute | solution.py:225
  12.6 9.7 %collective-permute-start.1 = (f32[1,2,192,256]{3,2,1,0:T(8,128)S(1)}, f32[1,2,192,256]{3,2,1,0:T(8,128)S(1)}, u32[]{:S(2)}, u32[]{:S(2)}) collective-permute-start(f32[1,2,192,256]{3,2,1,0:T(8,128)S(1)} %collective-permute-done.refs_1_), channel_id=1, source_target_pairs={{0,1},{1,0},{2,3},{3,2},{4,5},{5,4},{6,7},{7,6},{8,9},{9,8},{10,11... | collective-permute-start | bytes 1179656 | tf_op jit(solution)/shard_map/ppermute | solution.py:225
  16.5 15.6 %collective-permute-start.9 = (f32[1,2,192,256]{3,2,1,0:T(8,128)S(1)}, f32[1,2,192,256]{3,2,1,0:T(8,128)S(1)}, u32[]{:S(2)}, u32[]{:S(2)}) collective-permute-start(f32[1,2,192,256]{3,2,1,0:T(8,128)S(1)} %get-tuple-element.57), channel_id=1, source_target_pairs={{0,4},{1,0},{2,6},{3,2},{4,5},{5,1},{6,7},{7,3},{8,12},{9,8},{10,1... | collective-permute-start | bytes 1179656 | tf_op jit(solution)/shard_map/ppermute | solution.py:221
  16.6 17.5 %collective-permute-start.8 = (f32[1,2,192,256]{3,2,1,0:T(8,128)S(1)}, f32[1,2,192,256]{3,2,1,0:T(8,128)S(1)}, u32[]{:S(2)}, u32[]{:S(2)}) collective-permute-start(f32[1,2,192,256]{3,2,1,0:T(8,128)S(1)} %get-tuple-element.57), channel_id=1, source_target_pairs={{0,0},{1,4},{2,2},{3,6},{4,1},{5,5},{6,3},{7,7},{8,8},{9,12},{10,1... | collective-permute-start | bytes 1179656 | tf_op jit(solution)/shard_map/ppermute | solution.py:221
  21.0 14.4 %collective-permute-start.5 = (f32[1,2,192,256]{3,2,1,0:T(8,128)S(1)}, f32[1,2,192,256]{3,2,1,0:T(8,128)S(1)}, u32[]{:S(2)}, u32[]{:S(2)}) collective-permute-start(f32[1,2,192,256]{3,2,1,0:T(8,128)S(1)} %collective-permute-done.4.refs_1_), channel_id=1, source_target_pairs={{0,1},{1,0},{2,3},{3,2},{4,5},{5,4},{6,7},{7,6},{8,9},{9,8},{10,11... | collective-permute-start | bytes 1179656 | tf_op jit(solution)/shard_map/ppermute | solution.py:225
  25.1 10.9 %collective-permute-start.25 = (f32[2,256,128]{2,1,0:T(8,128)S(1)}, f32[2,256,128]{2,1,0:T(8,128)S(1)}, u32[]{:S(2)}, u32[]{:S(2)}) collective-permute-start(f32[2,256,128]{2,1,0:T(8,128)S(1)} %get-tuple-element.78), channel_id=1, source_target_pairs={{0,28},{1,29},{2,30},{3,31},{4,0},{5,1},{6,2},{7,3},{8,4},{9,5},{1... | collective-permute-start | bytes 786440 | tf_op jit(solution)/shard_map/ppermute | solution.py:221
  29.7 11.3 %collective-permute-start.14 = (f32[1,2,192,256]{3,2,1,0:T(8,128)S(1)}, f32[1,2,192,256]{3,2,1,0:T(8,128)S(1)}, u32[]{:S(2)}, u32[]{:S(2)}) collective-permute-start(f32[1,2,192,256]{3,2,1,0:T(8,128)S(1)} %get-tuple-element.63), channel_id=1, source_target_pairs={{0,4},{1,0},{2,6},{3,2},{4,5},{5,1},{6,7},{7,3},{8,12},{9,8},{10,1... | collective-permute-start | bytes 1179656 | tf_op jit(solution)/shard_map/ppermute | solution.py:221
  32.2 18.3 %collective-permute-start.13 = (f32[1,2,192,256]{3,2,1,0:T(8,128)S(1)}, f32[1,2,192,256]{3,2,1,0:T(8,128)S(1)}, u32[]{:S(2)}, u32[]{:S(2)}) collective-permute-start(f32[1,2,192,256]{3,2,1,0:T(8,128)S(1)} %get-tuple-element.63), channel_id=1, source_target_pairs={{0,0},{1,4},{2,2},{3,6},{4,1},{5,5},{6,3},{7,7},{8,8},{9,12},{10,1... | collective-permute-start | bytes 1179656 | tf_op jit(solution)/shard_map/ppermute | solution.py:221
  34.1 22.4 %collective-permute-start.11 = (f32[1,2,192,256]{3,2,1,0:T(8,128)S(1)}, f32[1,2,192,256]{3,2,1,0:T(8,128)S(1)}, u32[]{:S(2)}, u32[]{:S(2)}) collective-permute-start(f32[1,2,192,256]{3,2,1,0:T(8,128)S(1)} %collective-permute-done.9.refs_1_), channel_id=1, source_target_pairs={{0,2},{1,3},{2,0},{3,1},{4,6},{5,7},{6,4},{7,5},{8,10},{9,11},{10,... | collective-permute-start | bytes 1179656 | tf_op jit(solution)/shard_map/ppermute | solution.py:225
  35.4 10.5 %collective-permute-start.19 = (f32[2,256,128]{2,1,0:T(8,128)S(1)}, f32[2,256,128]{2,1,0:T(8,128)S(1)}, u32[]{:S(2)}, u32[]{:S(2)}) collective-permute-start(f32[2,256,128]{2,1,0:T(8,128)S(1)} %get-tuple-element.70), channel_id=1, source_target_pairs={{0,28},{1,29},{2,30},{3,31},{4,0},{5,1},{6,2},{7,3},{8,4},{9,5},{1... | collective-permute-start | bytes 786440 | tf_op jit(solution)/shard_map/ppermute | solution.py:221
  36.0 23.2 %collective-permute-start.10 = (f32[1,2,192,256]{3,2,1,0:T(8,128)S(1)}, f32[1,2,192,256]{3,2,1,0:T(8,128)S(1)}, u32[]{:S(2)}, u32[]{:S(2)}) collective-permute-start(f32[1,2,192,256]{3,2,1,0:T(8,128)S(1)} %collective-permute-done.8.refs_0_), channel_id=1, source_target_pairs={{0,2},{1,3},{2,0},{3,1},{4,6},{5,7},{6,4},{7,5},{8,10},{9,11},{10,... | collective-permute-start | bytes 1179656 | tf_op jit(solution)/shard_map/ppermute | solution.py:225
  41.0 21.1 %collective-permute-start.3 = (f32[2,256,128]{2,1,0:T(8,128)S(1)}, f32[2,256,128]{2,1,0:T(8,128)S(1)}, u32[]{:S(2)}, u32[]{:S(2)}) collective-permute-start(f32[2,256,128]{2,1,0:T(8,128)S(1)} %get-tuple-element.50), channel_id=1, source_target_pairs={{0,28},{1,29},{2,30},{3,31},{4,0},{5,1},{6,2},{7,3},{8,4},{9,5},{1... | collective-permute-start | bytes 786440 | tf_op jit(solution)/shard_map/ppermute | solution.py:221
  45.9 17.4 %collective-permute-start.26 = (f32[2,256,128]{2,1,0:T(8,128)S(1)}, f32[2,256,128]{2,1,0:T(8,128)S(1)}, u32[]{:S(2)}, u32[]{:S(2)}) collective-permute-start(f32[2,256,128]{2,1,0:T(8,128)S(1)} %get-tuple-element.79), channel_id=1, source_target_pairs={{0,1},{1,5},{2,3},{3,7},{4,8},{5,12},{6,10},{7,14},{8,9},{9,13},{1... | collective-permute-start | bytes 786440 | tf_op jit(solution)/shard_map/ppermute | solution.py:221
  50.5 15.9 %collective-permute-start.20 = (f32[2,256,128]{2,1,0:T(8,128)S(1)}, f32[2,256,128]{2,1,0:T(8,128)S(1)}, u32[]{:S(2)}, u32[]{:S(2)}) collective-permute-start(f32[2,256,128]{2,1,0:T(8,128)S(1)} %get-tuple-element.71), channel_id=1, source_target_pairs={{0,1},{1,5},{2,3},{3,7},{4,8},{5,12},{6,10},{7,14},{8,9},{9,13},{1... | collective-permute-start | bytes 786440 | tf_op jit(solution)/shard_map/ppermute | solution.py:221
  56.5 10.7 %collective-permute-start.21 = (f32[2,256,128]{2,1,0:T(8,128)S(1)}, f32[2,256,128]{2,1,0:T(8,128)S(1)}, u32[]{:S(2)}, u32[]{:S(2)}) collective-permute-start(f32[2,256,128]{2,1,0:T(8,128)S(1)} %get-tuple-element.72), channel_id=1, source_target_pairs={{0,0},{1,4},{2,2},{3,6},{4,1},{5,5},{6,3},{7,7},{8,8},{9,12},{10,1... | collective-permute-start | bytes 786440 | tf_op jit(solution)/shard_map/ppermute | solution.py:221
  59.2 14.8 %collective-permute-start.27 = (f32[2,256,128]{2,1,0:T(8,128)S(1)}, f32[2,256,128]{2,1,0:T(8,128)S(1)}, u32[]{:S(2)}, u32[]{:S(2)}) collective-permute-start(f32[2,256,128]{2,1,0:T(8,128)S(1)} %get-tuple-element.80), channel_id=1, source_target_pairs={{0,0},{1,4},{2,2},{3,6},{4,1},{5,5},{6,3},{7,7},{8,8},{9,12},{10,1... | collective-permute-start | bytes 786440 | tf_op jit(solution)/shard_map/ppermute | solution.py:221
  62.1 14.2 %collective-permute-start.16 = (f32[1,2,192,256]{3,2,1,0:T(8,128)S(1)}, f32[1,2,192,256]{3,2,1,0:T(8,128)S(1)}, u32[]{:S(2)}, u32[]{:S(2)}) collective-permute-start(f32[1,2,192,256]{3,2,1,0:T(8,128)S(1)} %collective-permute-done.14.refs_1_), channel_id=1, source_target_pairs={{0,2},{1,3},{2,0},{3,1},{4,6},{5,7},{6,4},{7,5},{8,10},{9,11},{10,... | collective-permute-start | bytes 1179656 | tf_op jit(solution)/shard_map/ppermute | solution.py:225
  63.3 18.3 %collective-permute-start.15 = (f32[1,2,192,256]{3,2,1,0:T(8,128)S(1)}, f32[1,2,192,256]{3,2,1,0:T(8,128)S(1)}, u32[]{:S(2)}, u32[]{:S(2)}) collective-permute-start(f32[1,2,192,256]{3,2,1,0:T(8,128)S(1)} %collective-permute-done.13.refs_0_), channel_id=1, source_target_pairs={{0,2},{1,3},{2,0},{3,1},{4,6},{5,7},{6,4},{7,5},{8,10},{9,11},{10,... | collective-permute-start | bytes 1179656 | tf_op jit(solution)/shard_map/ppermute | solution.py:225
  66.4 15.8 %collective-permute-start.6 = (f32[2,256,128]{2,1,0:T(8,128)S(1)}, f32[2,256,128]{2,1,0:T(8,128)S(1)}, u32[]{:S(2)}, u32[]{:S(2)}) collective-permute-start(f32[2,256,128]{2,1,0:T(8,128)S(1)} %get-tuple-element.55), channel_id=1, source_target_pairs={{0,1},{1,5},{2,3},{3,7},{4,8},{5,12},{6,10},{7,14},{8,9},{9,13},{1... | collective-permute-start | bytes 786440 | tf_op jit(solution)/shard_map/ppermute | solution.py:221
  67.2 15.0 %collective-permute-start.7 = (f32[2,256,128]{2,1,0:T(8,128)S(1)}, f32[2,256,128]{2,1,0:T(8,128)S(1)}, u32[]{:S(2)}, u32[]{:S(2)}) collective-permute-start(f32[2,256,128]{2,1,0:T(8,128)S(1)} %get-tuple-element.56), channel_id=1, source_target_pairs={{0,0},{1,4},{2,2},{3,6},{4,1},{5,5},{6,3},{7,7},{8,8},{9,12},{10,1... | collective-permute-start | bytes 786440 | tf_op jit(solution)/shard_map/ppermute | solution.py:221
  74.0 10.5 %collective-permute-start.22 = (f32[2,256,128]{2,1,0:T(8,128)S(1)}, f32[2,256,128]{2,1,0:T(8,128)S(1)}, u32[]{:S(2)}, u32[]{:S(2)}) collective-permute-start(f32[2,256,128]{2,1,0:T(8,128)S(1)} %get-tuple-element.74), channel_id=1, source_target_pairs={{0,25},{4,29},{2,27},{6,31},{1,0},{5,4},{3,2},{7,6},{8,1},{12,5},{... | collective-permute-start | bytes 786440 | tf_op jit(solution)/shard_map/ppermute | solution.py:221
  76.3 12.3 %collective-permute-start.28 = (f32[2,256,128]{2,1,0:T(8,128)S(1)}, f32[2,256,128]{2,1,0:T(8,128)S(1)}, u32[]{:S(2)}, u32[]{:S(2)}) collective-permute-start(f32[2,256,128]{2,1,0:T(8,128)S(1)} %get-tuple-element.82), channel_id=1, source_target_pairs={{0,25},{4,29},{2,27},{6,31},{1,0},{5,4},{3,2},{7,6},{8,1},{12,5},{... | collective-permute-start | bytes 786440 | tf_op jit(solution)/shard_map/ppermute | solution.py:221
  84.4 10.2 %collective-permute-start.12 = (f32[2,256,128]{2,1,0:T(8,128)S(1)}, f32[2,256,128]{2,1,0:T(8,128)S(1)}, u32[]{:S(2)}, u32[]{:S(2)}) collective-permute-start(f32[2,256,128]{2,1,0:T(8,128)S(1)} %get-tuple-element.62), channel_id=1, source_target_pairs={{0,25},{4,29},{2,27},{6,31},{1,0},{5,4},{3,2},{7,6},{8,1},{12,5},{... | collective-permute-start | bytes 786440 | tf_op jit(solution)/shard_map/ppermute | solution.py:221
  86.7 12.1 %collective-permute-start.23 = (f32[2,256,128]{2,1,0:T(8,128)S(1)}, f32[2,256,128]{2,1,0:T(8,128)S(1)}, u32[]{:S(2)}, u32[]{:S(2)}) collective-permute-start(f32[2,256,128]{2,1,0:T(8,128)S(1)} %get-tuple-element.75), channel_id=1, source_target_pairs={{0,0},{4,1},{2,2},{6,3},{1,4},{5,5},{3,6},{7,7},{8,8},{12,9},{10,1... | collective-permute-start | bytes 786440 | tf_op jit(solution)/shard_map/ppermute | solution.py:221
  90.8 21.1 %collective-permute-start.29 = (f32[2,256,128]{2,1,0:T(8,128)S(1)}, f32[2,256,128]{2,1,0:T(8,128)S(1)}, u32[]{:S(2)}, u32[]{:S(2)}) collective-permute-start(f32[2,256,128]{2,1,0:T(8,128)S(1)} %get-tuple-element.83), channel_id=1, source_target_pairs={{0,0},{4,1},{2,2},{6,3},{1,4},{5,5},{3,6},{7,7},{8,8},{12,9},{10,1... | collective-permute-start | bytes 786440 | tf_op jit(solution)/shard_map/ppermute | solution.py:221
  94.5 8.1 %collective-permute-start.24 = (f32[2,256,128]{2,1,0:T(8,128)S(1)}, f32[2,256,128]{2,1,0:T(8,128)S(1)}, u32[]{:S(2)}, u32[]{:S(2)}) collective-permute-start(f32[2,256,128]{2,1,0:T(8,128)S(1)} %get-tuple-element.76), channel_id=1, source_target_pairs={{0,4},{4,5},{2,6},{6,7},{1,8},{5,9},{3,10},{7,11},{8,12},{12,13},{... | collective-permute-start | bytes 786440 | tf_op jit(solution)/shard_map/ppermute | solution.py:221
  96.8 14.1 %collective-permute-start.17 = (f32[2,256,128]{2,1,0:T(8,128)S(1)}, f32[2,256,128]{2,1,0:T(8,128)S(1)}, u32[]{:S(2)}, u32[]{:S(2)}) collective-permute-start(f32[2,256,128]{2,1,0:T(8,128)S(1)} %get-tuple-element.67), channel_id=1, source_target_pairs={{0,0},{4,1},{2,2},{6,3},{1,4},{5,5},{3,6},{7,7},{8,8},{12,9},{10,1... | collective-permute-start | bytes 786440 | tf_op jit(solution)/shard_map/ppermute | solution.py:221
  98.7 12.2 %collective-permute-start.18 = (f32[2,256,128]{2,1,0:T(8,128)S(1)}, f32[2,256,128]{2,1,0:T(8,128)S(1)}, u32[]{:S(2)}, u32[]{:S(2)}) collective-permute-start(f32[2,256,128]{2,1,0:T(8,128)S(1)} %get-tuple-element.68), channel_id=1, source_target_pairs={{0,4},{4,5},{2,6},{6,7},{1,8},{5,9},{3,10},{7,11},{8,12},{12,13},{... | collective-permute-start | bytes 786440 | tf_op jit(solution)/shard_map/ppermute | solution.py:221
  98.8 13.1 %collective-permute-start.30 = (f32[2,256,128]{2,1,0:T(8,128)S(1)}, f32[2,256,128]{2,1,0:T(8,128)S(1)}, u32[]{:S(2)}, u32[]{:S(2)}) collective-permute-start(f32[2,256,128]{2,1,0:T(8,128)S(1)} %get-tuple-element.84), channel_id=1, source_target_pairs={{0,4},{4,5},{2,6},{6,7},{1,8},{5,9},{3,10},{7,11},{8,12},{12,13},{... | collective-permute-start | bytes 786440 | tf_op jit(solution)/shard_map/ppermute | solution.py:221

commit v2 on v1

--- a/solution.py
+++ b/solution.py
@@ -234,17 +234,23 @@
 
     operands = (block_order, reflectors, tri_factors)
     own = [None] * 4
-    (own[0],) = pack(*operands, [[0]])
-    own[2], own[3] = pack(*operands, [[2], [3]])
-    own[1], both = pack(*operands, [[1], [0, 1]])
+    own[0], own[2] = pack(*operands, [[0], [2]])
+    own[3], own[1], both = pack(*operands, [[3], [1], [0, 1]])
     partner = exchange(both, masks[-1])
     factors = []
     for tick in range(4):
         pieces = [(0, own[tick])]
         if tick >= 2:
-            pieces = [(f, move(own[tick], plain, swapped, flip=f)) for f in (0, masks[-1])]
-        for mask in masks[:-1]:
-            pieces = pieces + [(o ^ mask, exchange(p, mask)) for o, p in pieces]
+            pieces = []
+            for flip in (0, masks[-1]):
+                pieces.append((flip, move(own[tick], plain, swapped, flip=flip)))
+        spread = []
+        for piece in pieces:
+            group = [piece]
+            for mask in masks[:-1]:
+                group = group + [(o ^ mask, exchange(p, mask)) for o, p in group]
+            spread += group
+        pieces = spread
         if tick < 2:
             pieces += [(o ^ masks[-1], exchange(p, masks[-1])) for o, p in pieces[1:]]
         places = [(o, 0) for o, _ in pieces]

time: 113 us -> 113 us (level)
  waiting for transfers between devices: 20.8 us -> 22.4 us
  Pallas kernels: 36 us -> 34.6 us
    ppermute x9, waiting for transfers between devices: 6.24 us -> 7.88 us  [exchange(): lax.ppermute(block, 'cols', [(i, i ^ mask) for i in range(lax.axis_size('...]
    pallas_call x3 -> x2, Pallas kernels: 5.47 us -> 4.02 us  [pack(): pl.pallas_call(functools.partial(pack_kernel, groups), in_specs=[HBM, HBM...]
  transfers between devices with their start and end apart: 31 -> 31, of which waited for: 6 -> 6; matrix products, arithmetic and copies ran while one was open for 0% -> 0% of each run, Pallas kernels for 30% -> 28%
where the time goes in v2:
time: 113 us
  starting transfers between devices  55.5 us (49%)
  Pallas kernels  34.6 us (31%)
  waiting for transfers between devices  22.4 us (20%)
    ppermute x22, starting transfers between devices, move(): return lax.ppermute(value, ('rows', 'cols'), route)  45.7 us
    pallas_call x12, Pallas kernels, tick_call(): pl.pallas_call(functools.partial(tick_kernel, odd, swapped, chunk), in_sp...  26.5 us
    ppermute x22, waiting for transfers between devices, move(): return lax.ppermute(value, ('rows', 'cols'), route)  14.6 us
    ppermute x9, starting transfers between devices, exchange(): lax.ppermute(block, 'cols', [(i, i ^ mask) for i in range(lax.axis_size('...  9.83 us
    ppermute x9, waiting for transfers between devices, exchange(): lax.ppermute(block, 'cols', [(i, i ^ mask) for i in range(lax.axis_size('...  7.88 us
    pallas_call x2, Pallas kernels, pack(): pl.pallas_call(functools.partial(pack_kernel, groups), in_specs=[HBM, HBM...  4.02 us
  transfers between devices with their start and end apart: 31, of which 6 were waited for; matrix products, arithmetic and copies ran while one was open for 0% of the time, Pallas kernels for 28%

profile of v2, /device:TPU:1, one launch (start us, length us, event | category | flops | bytes accessed | tf_op | source)
XLA Modules:
  0.0 113.1 jit_solution(8352927507081950108)
XLA Ops:
  0.0 1.8 %pack.2 = (f32[1,2,192,256]{3,2,1,0:T(8,128)S(1)}, f32[1,2,192,256]{3,2,1,0:T(8,128)S(1)}) custom-call(s32[1,4]{1,0:T(1,128)} %order_hbm.3, f32[1,4,2,128,256]{4,3,2,1,0:T(8,128)} %v_ref.3, f32[1,4,2,64,256]{4,3,2,1,0:T(8,128)} %f_ref.3), custom_call_target="tpu_custom_call" | custom-call | tf_op jit(solution)/shard_map/pack/pallas_call | solution.py:53
  1.9 2.1 %collective-permute-start = (f32[1,2,192,256]{3,2,1,0:T(8,128)S(1)}, f32[1,2,192,256]{3,2,1,0:T(8,128)S(1)}, u32[]{:S(2)}, u32[]{:S(2)}) collective-permute-start(f32[1,2,192,256]{3,2,1,0:T(8,128)S(1)} %get-tuple-element.46.refs_0_), channel_id=1, source_target_pairs={{0,2},{1,3},{2,0},{3,1},{4,6},{5,7},{6,4},{7,5},{8,10},{9,11},{10,... | collective-permute-start | bytes 1179656 | tf_op jit(solution)/shard_map/ppermute | solution.py:225
  3.9 2.2 %pack.3 = (f32[1,2,192,256]{3,2,1,0:T(8,128)S(1)}, f32[1,2,192,256]{3,2,1,0:T(8,128)S(1)}, f32[2,2,192,256]{3,2,1,0:T(8,128)S(1)}) custom-call(s32[1,4]{1,0:T(1,128)} %order_hbm.3, f32[1,4,2,128,256]{4,3,2,1,0:T(8,128)} %v_ref.3, f32[1,4,2,64,256]{4,3,2,1,0:T(8,128)} %f_ref.3), custom_call_target="tpu_custom_call" | custom-call | tf_op jit(solution)/shard_map/pack/pallas_call | solution.py:53
  6.1 1.0 collective-permute-start.2
  7.2 5.6 %collective-permute-done.refs_1_ = f32[1,2,192,256]{3,2,1,0:T(8,128)S(1)} collective-permute-done((f32[1,2,192,256]{3,2,1,0:T(8,128)S(1)}, f32[1,2,192,256]{3,2,1,0:T(8,128)S(1)}, u32[]{:S(2)}, u32[]{:S(2)}) %collective-permute-start) | collective-permute-done | bytes 393248 | tf_op jit(solution)/shard_map/ppermute | solution.py:225
  12.8 2.1 %collective-permute-start.1 = (f32[1,2,192,256]{3,2,1,0:T(8,128)S(1)}, f32[1,2,192,256]{3,2,1,0:T(8,128)S(1)}, u32[]{:S(2)}, u32[]{:S(2)}) collective-permute-start(f32[1,2,192,256]{3,2,1,0:T(8,128)S(1)} %collective-permute-done.refs_1_), channel_id=1, source_target_pairs={{0,1},{1,0},{2,3},{3,2},{4,5},{5,4},{6,7},{7,6},{8,9},{9,8},{10,11... | collective-permute-start | bytes 1179656 | tf_op jit(solution)/shard_map/ppermute | solution.py:225
  14.9 4.1 %collective-permute-start.8 = (f32[1,2,192,256]{3,2,1,0:T(8,128)S(1)}, f32[1,2,192,256]{3,2,1,0:T(8,128)S(1)}, u32[]{:S(2)}, u32[]{:S(2)}) collective-permute-start(f32[1,2,192,256]{3,2,1,0:T(8,128)S(1)} %get-tuple-element.59), channel_id=1, source_target_pairs={{0,0},{1,4},{2,2},{3,6},{4,1},{5,5},{6,3},{7,7},{8,8},{9,12},{10,1... | collective-permute-start | bytes 1179656 | tf_op jit(solution)/shard_map/ppermute | solution.py:221
  18.9 2.3 %collective-permute-done.4.refs_1_ = f32[1,2,192,256]{3,2,1,0:T(8,128)S(1)} collective-permute-done((f32[1,2,192,256]{3,2,1,0:T(8,128)S(1)}, f32[1,2,192,256]{3,2,1,0:T(8,128)S(1)}, u32[]{:S(2)}, u32[]{:S(2)}) %collective-permute-start.4) | collective-permute-done | bytes 393248 | tf_op jit(solution)/shard_map/ppermute | solution.py:225
  21.2 1.3 %collective-permute-start.5 = (f32[1,2,192,256]{3,2,1,0:T(8,128)S(1)}, f32[1,2,192,256]{3,2,1,0:T(8,128)S(1)}, u32[]{:S(2)}, u32[]{:S(2)}) collective-permute-start(f32[1,2,192,256]{3,2,1,0:T(8,128)S(1)} %collective-permute-done.4.refs_1_), channel_id=1, source_target_pairs={{0,1},{1,0},{2,3},{3,2},{4,5},{5,4},{6,7},{7,6},{8,9},{9,8},{10,11... | collective-permute-start | bytes 1179656 | tf_op jit(solution)/shard_map/ppermute | solution.py:225
  22.4 0.6 prep.4
  23.0 2.2 %shard_map.54 = (f32[2,256,128]{2,1,0:T(8,128)S(1)}, f32[2,256,128]{2,1,0:T(8,128)S(1)}) custom-call(f32[2,512,384]{2,1,0:T(8,128)S(1)} %copy-done, f32[2,512,384]{2,1,0:T(8,128)S(1)} %copy-done, bf16[512,1024]{1,0:T(8,128)(2,1)S(1)} %get-tuple-element.48.refs_2_, bf16[1024,512]{1,0:T(8,128)(2,1)S(1)} %get-tuple-element.49.refs_3_, ...), custom_call_target="tpu_custom_call" | custom-call | flops 1006632960 | bytes 2621440 | tf_op jit(solution)/shard_map/pallas_call | solution.py:161
  25.2 4.6 %collective-permute-start.25 = (f32[2,256,128]{2,1,0:T(8,128)S(1)}, f32[2,256,128]{2,1,0:T(8,128)S(1)}, u32[]{:S(2)}, u32[]{:S(2)}) collective-permute-start(f32[2,256,128]{2,1,0:T(8,128)S(1)} %get-tuple-element.80), channel_id=1, source_target_pairs={{0,28},{1,29},{2,30},{3,31},{4,0},{5,1},{6,2},{7,3},{8,4},{9,5},{1... | collective-permute-start | bytes 786440 | tf_op jit(solution)/shard_map/ppermute | solution.py:221
  29.8 0.3 collective-permute-start.15
  30.1 2.2 %shard_map.50 = (f32[2,256,128]{2,1,0:T(8,128)S(1)}, f32[2,256,128]{2,1,0:T(8,128)S(1)}) custom-call(f32[2,512,384]{2,1,0:T(8,128)S(1)} %copy-done, f32[2,512,384]{2,1,0:T(8,128)S(1)} %copy-done, bf16[512,1024]{1,0:T(8,128)(2,1)S(1)} %get-tuple-element.48.refs_2_, bf16[1024,512]{1,0:T(8,128)(2,1)S(1)} %get-tuple-element.49.refs_3_, ...), custom_call_target="tpu_custom_call" | custom-call | flops 1006632960 | bytes 2621440 | tf_op jit(solution)/shard_map/pallas_call | solution.py:161
  32.3 1.9 %collective-permute-start.13 = (f32[1,2,192,256]{3,2,1,0:T(8,128)S(1)}, f32[1,2,192,256]{3,2,1,0:T(8,128)S(1)}, u32[]{:S(2)}, u32[]{:S(2)}) collective-permute-start(f32[1,2,192,256]{3,2,1,0:T(8,128)S(1)} %get-tuple-element.65), channel_id=1, source_target_pairs={{0,0},{1,4},{2,2},{3,6},{4,1},{5,5},{6,3},{7,7},{8,8},{9,12},{10,1... | collective-permute-start | bytes 1179656 | tf_op jit(solution)/shard_map/ppermute | solution.py:221
  34.3 1.3 %collective-permute-start.11 = (f32[1,2,192,256]{3,2,1,0:T(8,128)S(1)}, f32[1,2,192,256]{3,2,1,0:T(8,128)S(1)}, u32[]{:S(2)}, u32[]{:S(2)}) collective-permute-start(f32[1,2,192,256]{3,2,1,0:T(8,128)S(1)} %collective-permute-done.10.refs_2_), channel_id=1, source_target_pairs={{0,2},{1,3},{2,0},{3,1},{4,6},{5,7},{6,4},{7,5},{8,10},{9,11},{10,... | collective-permute-start | bytes 1179656 | tf_op jit(solution)/shard_map/ppermute | solution.py:225
  35.6 0.6 prep.5
  36.1 0.6 collective-permute-start.9
  36.7 2.2 %shard_map.46 = (f32[2,256,128]{2,1,0:T(8,128)S(1)}, f32[2,256,128]{2,1,0:T(8,128)S(1)}) custom-call(f32[2,512,384]{2,1,0:T(8,128)S(1)} %copy-done, f32[2,512,384]{2,1,0:T(8,128)S(1)} %copy-done, bf16[512,1024]{1,0:T(8,128)(2,1)S(1)} %get-tuple-element.48.refs_2_, bf16[1024,512]{1,0:T(8,128)(2,1)S(1)} %get-tuple-element.49.refs_3_, ...), custom_call_target="tpu_custom_call" | custom-call | flops 1006632960 | bytes 2621440 | tf_op jit(solution)/shard_map/pallas_call | solution.py:161
  38.9 2.2 %shard_map.55 = (f32[2,256,128]{2,1,0:T(8,128)S(1)}, f32[2,256,128]{2,1,0:T(8,128)S(1)}) custom-call(f32[2,256,128]{2,1,0:T(8,128)S(1)} %get-tuple-element.79.refs_0_, f32[2,256,128]{2,1,0:T(8,128)S(1)} %collective-permute-done.25.refs_1_, bf16[512,1024]{1,0:T(8,128)(2,1)S(1)} %get-tuple-element.54.refs_2_, bf16[1024,512]{1,0:T(8,128)(2,1)S(1)} %get-tuple-element.55.refs_3_, ...), custom_call_target="tpu_custom_call" | custom-call | flops 1006632960 | bytes 2621440 | tf_op jit(solution)/shard_map/pallas_call | solution.py:161
  41.1 4.9 %collective-permute-start.3 = (f32[2,256,128]{2,1,0:T(8,128)S(1)}, f32[2,256,128]{2,1,0:T(8,128)S(1)}, u32[]{:S(2)}, u32[]{:S(2)}) collective-permute-start(f32[2,256,128]{2,1,0:T(8,128)S(1)} %get-tuple-element.52), channel_id=1, source_target_pairs={{0,28},{1,29},{2,30},{3,31},{4,0},{5,1},{6,2},{7,3},{8,4},{9,5},{1... | collective-permute-start | bytes 786440 | tf_op jit(solution)/shard_map/ppermute | solution.py:221
  46.1 2.2 %shard_map.51 = (f32[2,256,128]{2,1,0:T(8,128)S(1)}, f32[2,256,128]{2,1,0:T(8,128)S(1)}) custom-call(f32[2,256,128]{2,1,0:T(8,128)S(1)} %get-tuple-element.71.refs_0_, f32[2,256,128]{2,1,0:T(8,128)S(1)} %collective-permute-done.19.refs_1_, bf16[512,1024]{1,0:T(8,128)(2,1)S(1)} %get-tuple-element.54.refs_2_, bf16[1024,512]{1,0:T(8,128)(2,1)S(1)} %get-tuple-element.55.refs_3_, ...), custom_call_target="tpu_custom_call" | custom-call | flops 1006632960 | bytes 2621440 | tf_op jit(solution)/shard_map/pallas_call | solution.py:161
  48.3 2.4 %collective-permute-done.13.refs_0_ = f32[1,2,192,256]{3,2,1,0:T(8,128)S(1)} collective-permute-done((f32[1,2,192,256]{3,2,1,0:T(8,128)S(1)}, f32[1,2,192,256]{3,2,1,0:T(8,128)S(1)}, u32[]{:S(2)}, u32[]{:S(2)}) %collective-permute-start.13) | collective-permute-done | bytes 393248 | tf_op jit(solution)/shard_map/ppermute | solution.py:221
  50.7 6.0 %collective-permute-start.20 = (f32[2,256,128]{2,1,0:T(8,128)S(1)}, f32[2,256,128]{2,1,0:T(8,128)S(1)}, u32[]{:S(2)}, u32[]{:S(2)}) collective-permute-start(f32[2,256,128]{2,1,0:T(8,128)S(1)} %get-tuple-element.73), channel_id=1, source_target_pairs={{0,1},{1,5},{2,3},{3,7},{4,8},{5,12},{6,10},{7,14},{8,9},{9,13},{1... | collective-permute-start | bytes 786440 | tf_op jit(solution)/shard_map/ppermute | solution.py:221
  56.6 2.7 %collective-permute-start.21 = (f32[2,256,128]{2,1,0:T(8,128)S(1)}, f32[2,256,128]{2,1,0:T(8,128)S(1)}, u32[]{:S(2)}, u32[]{:S(2)}) collective-permute-start(f32[2,256,128]{2,1,0:T(8,128)S(1)} %get-tuple-element.74), channel_id=1, source_target_pairs={{0,0},{1,4},{2,2},{3,6},{4,1},{5,5},{6,3},{7,7},{8,8},{9,12},{10,1... | collective-permute-start | bytes 786440 | tf_op jit(solution)/shard_map/ppermute | solution.py:221
  59.4 2.8 %collective-permute-start.27 = (f32[2,256,128]{2,1,0:T(8,128)S(1)}, f32[2,256,128]{2,1,0:T(8,128)S(1)}, u32[]{:S(2)}, u32[]{:S(2)}) collective-permute-start(f32[2,256,128]{2,1,0:T(8,128)S(1)} %get-tuple-element.82), channel_id=1, source_target_pairs={{0,0},{1,4},{2,2},{3,6},{4,1},{5,5},{6,3},{7,7},{8,8},{9,12},{10,1... | collective-permute-start | bytes 786440 | tf_op jit(solution)/shard_map/ppermute | solution.py:221
  62.2 1.3 %collective-permute-start.16 = (f32[1,2,192,256]{3,2,1,0:T(8,128)S(1)}, f32[1,2,192,256]{3,2,1,0:T(8,128)S(1)}, u32[]{:S(2)}, u32[]{:S(2)}) collective-permute-start(f32[1,2,192,256]{3,2,1,0:T(8,128)S(1)} %collective-permute-done.15.refs_2_), channel_id=1, source_target_pairs={{0,2},{1,3},{2,0},{3,1},{4,6},{5,7},{6,4},{7,5},{8,10},{9,11},{10,... | collective-permute-start | bytes 1179656 | tf_op jit(solution)/shard_map/ppermute | solution.py:225
  63.5 0.3 collective-permute-start.14
  63.8 0.6 prep.6
  64.3 2.2 %shard_map.47 = (f32[2,256,128]{2,1,0:T(8,128)S(1)}, f32[2,256,128]{2,1,0:T(8,128)S(1)}) custom-call(f32[2,256,128]{2,1,0:T(8,128)S(1)} %get-tuple-element.51.refs_0_, f32[2,256,128]{2,1,0:T(8,128)S(1)} %collective-permute-done.3.refs_1_, bf16[512,1024]{1,0:T(8,128)(2,1)S(1)} %get-tuple-element.54.refs_2_, bf16[1024,512]{1,0:T(8,128)(2,1)S(1)} %get-tuple-element.55.refs_3_, ...), custom_call_target="tpu_custom_call" | custom-call | flops 1006632960 | bytes 2621440 | tf_op jit(solution)/shard_map/pallas_call | solution.py:161
  66.6 0.7 collective-permute-done.21.refs_1_
  67.4 4.6 %collective-permute-start.7 = (f32[2,256,128]{2,1,0:T(8,128)S(1)}, f32[2,256,128]{2,1,0:T(8,128)S(1)}, u32[]{:S(2)}, u32[]{:S(2)}) collective-permute-start(f32[2,256,128]{2,1,0:T(8,128)S(1)} %get-tuple-element.58), channel_id=1, source_target_pairs={{0,0},{1,4},{2,2},{3,6},{4,1},{5,5},{6,3},{7,7},{8,8},{9,12},{10,1... | collective-permute-start | bytes 786440 | tf_op jit(solution)/shard_map/ppermute | solution.py:221
  71.9 2.2 %shard_map.52 = (f32[2,256,128]{2,1,0:T(8,128)S(1)}, f32[2,256,128]{2,1,0:T(8,128)S(1)}) custom-call(f32[2,256,128]{2,1,0:T(8,128)S(1)} %collective-permute-done.20.refs_0_, f32[2,256,128]{2,1,0:T(8,128)S(1)} %collective-permute-done.21.refs_1_, bf16[512,1024]{1,0:T(8,128)(2,1)S(1)} %get-tuple-element.60.refs_2_, ...), custom_call_target="tpu_custom_call" | custom-call | flops 1006632960 | bytes 2621440 | tf_op jit(solution)/shard_map/pallas_call | solution.py:161
  74.2 2.2 %shard_map.56 = (f32[2,256,128]{2,1,0:T(8,128)S(1)}, f32[2,256,128]{2,1,0:T(8,128)S(1)}) custom-call(f32[2,256,128]{2,1,0:T(8,128)S(1)} %collective-permute-done.26.refs_0_, f32[2,256,128]{2,1,0:T(8,128)S(1)} %collective-permute-done.27.refs_1_, bf16[512,1024]{1,0:T(8,128)(2,1)S(1)} %get-tuple-element.60.refs_2_, ...), custom_call_target="tpu_custom_call" | custom-call | flops 1006632960 | bytes 2621440 | tf_op jit(solution)/shard_map/pallas_call | solution.py:161
  76.5 5.3 %collective-permute-start.28 = (f32[2,256,128]{2,1,0:T(8,128)S(1)}, f32[2,256,128]{2,1,0:T(8,128)S(1)}, u32[]{:S(2)}, u32[]{:S(2)}) collective-permute-start(f32[2,256,128]{2,1,0:T(8,128)S(1)} %get-tuple-element.84), channel_id=1, source_target_pairs={{0,25},{4,29},{2,27},{6,31},{1,0},{5,4},{3,2},{7,6},{8,1},{12,5},{... | collective-permute-start | bytes 786440 | tf_op jit(solution)/shard_map/ppermute | solution.py:221
  81.8 0.6 prep.7
  82.4 2.2 %shard_map.48 = (f32[2,256,128]{2,1,0:T(8,128)S(1)}, f32[2,256,128]{2,1,0:T(8,128)S(1)}) custom-call(f32[2,256,128]{2,1,0:T(8,128)S(1)} %collective-permute-done.6.refs_0_, f32[2,256,128]{2,1,0:T(8,128)S(1)} %collective-permute-done.7.refs_1_, bf16[512,1024]{1,0:T(8,128)(2,1)S(1)} %get-tuple-element.60.refs_2_, ...), custom_call_target="tpu_custom_call" | custom-call | flops 1006632960 | bytes 2621440 | tf_op jit(solution)/shard_map/pallas_call | solution.py:161
  84.6 2.2 %shard_map.53 = (f32[2,256,128]{2,1,0:T(8,128)S(1)}, f32[2,256,128]{2,1,0:T(8,128)S(1)}) custom-call(f32[2,256,128]{2,1,0:T(8,128)S(1)} %get-tuple-element.75.refs_0_, f32[2,256,128]{2,1,0:T(8,128)S(1)} %collective-permute-done.22.refs_1_, bf16[512,1024]{1,0:T(8,128)(2,1)S(1)} %get-tuple-element.66.refs_2_, bf16[1024,512]{1,0:T(8,128)(2,1)S(1)} %get-tuple-element.67.refs_3_, ...), custom_call_target="tpu_custom_call" | custom-call | flops 1006632960 | bytes 2621440 | tf_op jit(solution)/shard_map/pallas_call | solution.py:161
  86.9 1.9 %collective-permute-start.23 = (f32[2,256,128]{2,1,0:T(8,128)S(1)}, f32[2,256,128]{2,1,0:T(8,128)S(1)}, u32[]{:S(2)}, u32[]{:S(2)}) collective-permute-start(f32[2,256,128]{2,1,0:T(8,128)S(1)} %get-tuple-element.77), channel_id=1, source_target_pairs={{0,0},{4,1},{2,2},{6,3},{1,4},{5,5},{3,6},{7,7},{8,8},{12,9},{10,1... | collective-permute-start | bytes 786440 | tf_op jit(solution)/shard_map/ppermute | solution.py:221
  88.8 2.2 %shard_map.57 = (f32[2,256,128]{2,1,0:T(8,128)S(1)}, f32[2,256,128]{2,1,0:T(8,128)S(1)}) custom-call(f32[2,256,128]{2,1,0:T(8,128)S(1)} %get-tuple-element.83.refs_0_, f32[2,256,128]{2,1,0:T(8,128)S(1)} %collective-permute-done.28.refs_1_, bf16[512,1024]{1,0:T(8,128)(2,1)S(1)} %get-tuple-element.66.refs_2_, bf16[1024,512]{1,0:T(8,128)(2,1)S(1)} %get-tuple-element.67.refs_3_, ...), custom_call_target="tpu_custom_call" | custom-call | flops 1006632960 | bytes 2621440 | tf_op jit(solution)/shard_map/pallas_call | solution.py:161
  91.0 3.6 %collective-permute-start.29 = (f32[2,256,128]{2,1,0:T(8,128)S(1)}, f32[2,256,128]{2,1,0:T(8,128)S(1)}, u32[]{:S(2)}, u32[]{:S(2)}) collective-permute-start(f32[2,256,128]{2,1,0:T(8,128)S(1)} %get-tuple-element.85), channel_id=1, source_target_pairs={{0,0},{4,1},{2,2},{6,3},{1,4},{5,5},{3,6},{7,7},{8,8},{12,9},{10,1... | collective-permute-start | bytes 786440 | tf_op jit(solution)/shard_map/ppermute | solution.py:221
  94.8 2.2 %shard_map.49 = (f32[2,256,128]{2,1,0:T(8,128)S(1)}, f32[2,256,128]{2,1,0:T(8,128)S(1)}) custom-call(f32[2,256,128]{2,1,0:T(8,128)S(1)} %get-tuple-element.63.refs_0_, f32[2,256,128]{2,1,0:T(8,128)S(1)} %collective-permute-done.12.refs_1_, bf16[512,1024]{1,0:T(8,128)(2,1)S(1)} %get-tuple-element.66.refs_2_, bf16[1024,512]{1,0:T(8,128)(2,1)S(1)} %get-tuple-element.67.refs_3_, ...), custom_call_target="tpu_custom_call" | custom-call | flops 1006632960 | bytes 2621440 | tf_op jit(solution)/shard_map/pallas_call | solution.py:161
  97.0 1.9 %collective-permute-start.17 = (f32[2,256,128]{2,1,0:T(8,128)S(1)}, f32[2,256,128]{2,1,0:T(8,128)S(1)}, u32[]{:S(2)}, u32[]{:S(2)}) collective-permute-start(f32[2,256,128]{2,1,0:T(8,128)S(1)} %get-tuple-element.69), channel_id=1, source_target_pairs={{0,0},{4,1},{2,2},{6,3},{1,4},{5,5},{3,6},{7,7},{8,8},{12,9},{10,1... | collective-permute-start | bytes 786440 | tf_op jit(solution)/shard_map/ppermute | solution.py:221
  99.0 0.6 collective-permute-start.30
  99.6 3.1 %collective-permute-done.24.refs_3_ = f32[2,256,128]{2,1,0:T(8,128)S(1)} collective-permute-done((f32[2,256,128]{2,1,0:T(8,128)S(1)}, f32[2,256,128]{2,1,0:T(8,128)S(1)}, u32[]{:S(2)}, u32[]{:S(2)}) %collective-permute-start.24) | collective-permute-done | bytes 262176 | tf_op jit(solution)/shard_map/ppermute | solution.py:221
  102.7 8.3 %collective-permute-done.17.refs_0_ = f32[2,256,128]{2,1,0:T(8,128)S(1)} collective-permute-done((f32[2,256,128]{2,1,0:T(8,128)S(1)}, f32[2,256,128]{2,1,0:T(8,128)S(1)}, u32[]{:S(2)}, u32[]{:S(2)}) %collective-permute-start.17) | collective-permute-done | bytes 262176 | tf_op jit(solution)/shard_map/ppermute | solution.py:221
  111.1 1.0 finish.2.refs_0_
  112.1 0.8 finish.3
  (36 shorter events, 0.4 us)
Async XLA Ops:
  1.8 21.2 %copy-start = (f32[2,512,384]{2,1,0:T(8,128)S(1)}, f32[2,512,384]{2,1,0:T(8,128)}, u32[]{:S(2)}) copy-start(f32[2,512,384]{2,1,0:T(8,128)} %refs_1_.5) | copy-start | bytes 4718596
  1.9 10.9 %collective-permute-start = (f32[1,2,192,256]{3,2,1,0:T(8,128)S(1)}, f32[1,2,192,256]{3,2,1,0:T(8,128)S(1)}, u32[]{:S(2)}, u32[]{:S(2)}) collective-permute-start(f32[1,2,192,256]{3,2,1,0:T(8,128)S(1)} %get-tuple-element.46.refs_0_), channel_id=1, source_target_pairs={{0,2},{1,3},{2,0},{3,1},{4,6},{5,7},{6,4},{7,5},{8,10},{9,11},{10,... | collective-permute-start | bytes 1179656 | tf_op jit(solution)/shard_map/ppermute | solution.py:225
  6.1 16.3 %collective-permute-start.2 = (f32[2,2,192,256]{3,2,1,0:T(8,128)S(1)}, f32[2,2,192,256]{3,2,1,0:T(8,128)S(1)}, u32[]{:S(2)}, u32[]{:S(2)}) collective-permute-start(f32[2,2,192,256]{3,2,1,0:T(8,128)S(1)} %get-tuple-element.47), channel_id=1, source_target_pairs={{0,1},{1,0},{2,3},{3,2},{4,5},{5,4},{6,7},{7,6},{8,9},{9,8},{10,11... | collective-permute-start | bytes 2359304 | tf_op jit(solution)/shard_map/ppermute | solution.py:225
  7.2 14.0 %collective-permute-start.4 = (f32[1,2,192,256]{3,2,1,0:T(8,128)S(1)}, f32[1,2,192,256]{3,2,1,0:T(8,128)S(1)}, u32[]{:S(2)}, u32[]{:S(2)}) collective-permute-start(f32[1,2,192,256]{3,2,1,0:T(8,128)S(1)} %get-tuple-element.53.refs_0_), channel_id=1, source_target_pairs={{0,2},{1,3},{2,0},{3,1},{4,6},{5,7},{6,4},{7,5},{8,10},{9,11},{10,... | collective-permute-start | bytes 1179656 | tf_op jit(solution)/shard_map/ppermute | solution.py:225
  12.8 9.7 %collective-permute-start.1 = (f32[1,2,192,256]{3,2,1,0:T(8,128)S(1)}, f32[1,2,192,256]{3,2,1,0:T(8,128)S(1)}, u32[]{:S(2)}, u32[]{:S(2)}) collective-permute-start(f32[1,2,192,256]{3,2,1,0:T(8,128)S(1)} %collective-permute-done.refs_1_), channel_id=1, source_target_pairs={{0,1},{1,0},{2,3},{3,2},{4,5},{5,4},{6,7},{7,6},{8,9},{9,8},{10,11... | collective-permute-start | bytes 1179656 | tf_op jit(solution)/shard_map/ppermute | solution.py:225
  14.9 17.5 %collective-permute-start.10 = (f32[1,2,192,256]{3,2,1,0:T(8,128)S(1)}, f32[1,2,192,256]{3,2,1,0:T(8,128)S(1)}, u32[]{:S(2)}, u32[]{:S(2)}) collective-permute-start(f32[1,2,192,256]{3,2,1,0:T(8,128)S(1)} %get-tuple-element.59), channel_id=1, source_target_pairs={{0,4},{1,0},{2,6},{3,2},{4,5},{5,1},{6,7},{7,3},{8,12},{9,8},{10,1... | collective-permute-start | bytes 1179656 | tf_op jit(solution)/shard_map/ppermute | solution.py:221
  14.9 19.4 %collective-permute-start.8 = (f32[1,2,192,256]{3,2,1,0:T(8,128)S(1)}, f32[1,2,192,256]{3,2,1,0:T(8,128)S(1)}, u32[]{:S(2)}, u32[]{:S(2)}) collective-permute-start(f32[1,2,192,256]{3,2,1,0:T(8,128)S(1)} %get-tuple-element.59), channel_id=1, source_target_pairs={{0,0},{1,4},{2,2},{3,6},{4,1},{5,5},{6,3},{7,7},{8,8},{9,12},{10,1... | collective-permute-start | bytes 1179656 | tf_op jit(solution)/shard_map/ppermute | solution.py:221
  21.2 14.4 %collective-permute-start.5 = (f32[1,2,192,256]{3,2,1,0:T(8,128)S(1)}, f32[1,2,192,256]{3,2,1,0:T(8,128)S(1)}, u32[]{:S(2)}, u32[]{:S(2)}) collective-permute-start(f32[1,2,192,256]{3,2,1,0:T(8,128)S(1)} %collective-permute-done.4.refs_1_), channel_id=1, source_target_pairs={{0,1},{1,0},{2,3},{3,2},{4,5},{5,4},{6,7},{7,6},{8,9},{9,8},{10,11... | collective-permute-start | bytes 1179656 | tf_op jit(solution)/shard_map/ppermute | solution.py:225
  25.2 10.9 %collective-permute-start.25 = (f32[2,256,128]{2,1,0:T(8,128)S(1)}, f32[2,256,128]{2,1,0:T(8,128)S(1)}, u32[]{:S(2)}, u32[]{:S(2)}) collective-permute-start(f32[2,256,128]{2,1,0:T(8,128)S(1)} %get-tuple-element.80), channel_id=1, source_target_pairs={{0,28},{1,29},{2,30},{3,31},{4,0},{5,1},{6,2},{7,3},{8,4},{9,5},{1... | collective-permute-start | bytes 786440 | tf_op jit(solution)/shard_map/ppermute | solution.py:221
  29.8 11.3 %collective-permute-start.15 = (f32[1,2,192,256]{3,2,1,0:T(8,128)S(1)}, f32[1,2,192,256]{3,2,1,0:T(8,128)S(1)}, u32[]{:S(2)}, u32[]{:S(2)}) collective-permute-start(f32[1,2,192,256]{3,2,1,0:T(8,128)S(1)} %get-tuple-element.65), channel_id=1, source_target_pairs={{0,4},{1,0},{2,6},{3,2},{4,5},{5,1},{6,7},{7,3},{8,12},{9,8},{10,1... | collective-permute-start | bytes 1179656 | tf_op jit(solution)/shard_map/ppermute | solution.py:221
  32.3 18.3 %collective-permute-start.13 = (f32[1,2,192,256]{3,2,1,0:T(8,128)S(1)}, f32[1,2,192,256]{3,2,1,0:T(8,128)S(1)}, u32[]{:S(2)}, u32[]{:S(2)}) collective-permute-start(f32[1,2,192,256]{3,2,1,0:T(8,128)S(1)} %get-tuple-element.65), channel_id=1, source_target_pairs={{0,0},{1,4},{2,2},{3,6},{4,1},{5,5},{6,3},{7,7},{8,8},{9,12},{10,1... | collective-permute-start | bytes 1179656 | tf_op jit(solution)/shard_map/ppermute | solution.py:221
  34.3 22.4 %collective-permute-start.11 = (f32[1,2,192,256]{3,2,1,0:T(8,128)S(1)}, f32[1,2,192,256]{3,2,1,0:T(8,128)S(1)}, u32[]{:S(2)}, u32[]{:S(2)}) collective-permute-start(f32[1,2,192,256]{3,2,1,0:T(8,128)S(1)} %collective-permute-done.10.refs_2_), channel_id=1, source_target_pairs={{0,2},{1,3},{2,0},{3,1},{4,6},{5,7},{6,4},{7,5},{8,10},{9,11},{10,... | collective-permute-start | bytes 1179656 | tf_op jit(solution)/shard_map/ppermute | solution.py:225
  35.6 10.5 %collective-permute-start.19 = (f32[2,256,128]{2,1,0:T(8,128)S(1)}, f32[2,256,128]{2,1,0:T(8,128)S(1)}, u32[]{:S(2)}, u32[]{:S(2)}) collective-permute-start(f32[2,256,128]{2,1,0:T(8,128)S(1)} %get-tuple-element.72), channel_id=1, source_target_pairs={{0,28},{1,29},{2,30},{3,31},{4,0},{5,1},{6,2},{7,3},{8,4},{9,5},{1... | collective-permute-start | bytes 786440 | tf_op jit(solution)/shard_map/ppermute | solution.py:221
  36.1 23.2 %collective-permute-start.9 = (f32[1,2,192,256]{3,2,1,0:T(8,128)S(1)}, f32[1,2,192,256]{3,2,1,0:T(8,128)S(1)}, u32[]{:S(2)}, u32[]{:S(2)}) collective-permute-start(f32[1,2,192,256]{3,2,1,0:T(8,128)S(1)} %collective-permute-done.8.refs_0_), channel_id=1, source_target_pairs={{0,2},{1,3},{2,0},{3,1},{4,6},{5,7},{6,4},{7,5},{8,10},{9,11},{10,... | collective-permute-start | bytes 1179656 | tf_op jit(solution)/shard_map/ppermute | solution.py:225
  41.1 21.1 %collective-permute-start.3 = (f32[2,256,128]{2,1,0:T(8,128)S(1)}, f32[2,256,128]{2,1,0:T(8,128)S(1)}, u32[]{:S(2)}, u32[]{:S(2)}) collective-permute-start(f32[2,256,128]{2,1,0:T(8,128)S(1)} %get-tuple-element.52), channel_id=1, source_target_pairs={{0,28},{1,29},{2,30},{3,31},{4,0},{5,1},{6,2},{7,3},{8,4},{9,5},{1... | collective-permute-start | bytes 786440 | tf_op jit(solution)/shard_map/ppermute | solution.py:221
  46.1 17.4 %collective-permute-start.26 = (f32[2,256,128]{2,1,0:T(8,128)S(1)}, f32[2,256,128]{2,1,0:T(8,128)S(1)}, u32[]{:S(2)}, u32[]{:S(2)}) collective-permute-start(f32[2,256,128]{2,1,0:T(8,128)S(1)} %get-tuple-element.81), channel_id=1, source_target_pairs={{0,1},{1,5},{2,3},{3,7},{4,8},{5,12},{6,10},{7,14},{8,9},{9,13},{1... | collective-permute-start | bytes 786440 | tf_op jit(solution)/shard_map/ppermute | solution.py:221
  50.7 15.9 %collective-permute-start.20 = (f32[2,256,128]{2,1,0:T(8,128)S(1)}, f32[2,256,128]{2,1,0:T(8,128)S(1)}, u32[]{:S(2)}, u32[]{:S(2)}) collective-permute-start(f32[2,256,128]{2,1,0:T(8,128)S(1)} %get-tuple-element.73), channel_id=1, source_target_pairs={{0,1},{1,5},{2,3},{3,7},{4,8},{5,12},{6,10},{7,14},{8,9},{9,13},{1... | collective-permute-start | bytes 786440 | tf_op jit(solution)/shard_map/ppermute | solution.py:221
  56.6 10.7 %collective-permute-start.21 = (f32[2,256,128]{2,1,0:T(8,128)S(1)}, f32[2,256,128]{2,1,0:T(8,128)S(1)}, u32[]{:S(2)}, u32[]{:S(2)}) collective-permute-start(f32[2,256,128]{2,1,0:T(8,128)S(1)} %get-tuple-element.74), channel_id=1, source_target_pairs={{0,0},{1,4},{2,2},{3,6},{4,1},{5,5},{6,3},{7,7},{8,8},{9,12},{10,1... | collective-permute-start | bytes 786440 | tf_op jit(solution)/shard_map/ppermute | solution.py:221
  59.4 14.8 %collective-permute-start.27 = (f32[2,256,128]{2,1,0:T(8,128)S(1)}, f32[2,256,128]{2,1,0:T(8,128)S(1)}, u32[]{:S(2)}, u32[]{:S(2)}) collective-permute-start(f32[2,256,128]{2,1,0:T(8,128)S(1)} %get-tuple-element.82), channel_id=1, source_target_pairs={{0,0},{1,4},{2,2},{3,6},{4,1},{5,5},{6,3},{7,7},{8,8},{9,12},{10,1... | collective-permute-start | bytes 786440 | tf_op jit(solution)/shard_map/ppermute | solution.py:221
  62.2 14.2 %collective-permute-start.16 = (f32[1,2,192,256]{3,2,1,0:T(8,128)S(1)}, f32[1,2,192,256]{3,2,1,0:T(8,128)S(1)}, u32[]{:S(2)}, u32[]{:S(2)}) collective-permute-start(f32[1,2,192,256]{3,2,1,0:T(8,128)S(1)} %collective-permute-done.15.refs_2_), channel_id=1, source_target_pairs={{0,2},{1,3},{2,0},{3,1},{4,6},{5,7},{6,4},{7,5},{8,10},{9,11},{10,... | collective-permute-start | bytes 1179656 | tf_op jit(solution)/shard_map/ppermute | solution.py:225
  63.5 18.2 %collective-permute-start.14 = (f32[1,2,192,256]{3,2,1,0:T(8,128)S(1)}, f32[1,2,192,256]{3,2,1,0:T(8,128)S(1)}, u32[]{:S(2)}, u32[]{:S(2)}) collective-permute-start(f32[1,2,192,256]{3,2,1,0:T(8,128)S(1)} %collective-permute-done.13.refs_0_), channel_id=1, source_target_pairs={{0,2},{1,3},{2,0},{3,1},{4,6},{5,7},{6,4},{7,5},{8,10},{9,11},{10,... | collective-permute-start | bytes 1179656 | tf_op jit(solution)/shard_map/ppermute | solution.py:225
  66.6 15.8 %collective-permute-start.6 = (f32[2,256,128]{2,1,0:T(8,128)S(1)}, f32[2,256,128]{2,1,0:T(8,128)S(1)}, u32[]{:S(2)}, u32[]{:S(2)}) collective-permute-start(f32[2,256,128]{2,1,0:T(8,128)S(1)} %get-tuple-element.57), channel_id=1, source_target_pairs={{0,1},{1,5},{2,3},{3,7},{4,8},{5,12},{6,10},{7,14},{8,9},{9,13},{1... | collective-permute-start | bytes 786440 | tf_op jit(solution)/shard_map/ppermute | solution.py:221
  67.4 15.0 %collective-permute-start.7 = (f32[2,256,128]{2,1,0:T(8,128)S(1)}, f32[2,256,128]{2,1,0:T(8,128)S(1)}, u32[]{:S(2)}, u32[]{:S(2)}) collective-permute-start(f32[2,256,128]{2,1,0:T(8,128)S(1)} %get-tuple-element.58), channel_id=1, source_target_pairs={{0,0},{1,4},{2,2},{3,6},{4,1},{5,5},{6,3},{7,7},{8,8},{9,12},{10,1... | collective-permute-start | bytes 786440 | tf_op jit(solution)/shard_map/ppermute | solution.py:221
  74.2 10.5 %collective-permute-start.22 = (f32[2,256,128]{2,1,0:T(8,128)S(1)}, f32[2,256,128]{2,1,0:T(8,128)S(1)}, u32[]{:S(2)}, u32[]{:S(2)}) collective-permute-start(f32[2,256,128]{2,1,0:T(8,128)S(1)} %get-tuple-element.76), channel_id=1, source_target_pairs={{0,25},{4,29},{2,27},{6,31},{1,0},{5,4},{3,2},{7,6},{8,1},{12,5},{... | collective-permute-start | bytes 786440 | tf_op jit(solution)/shard_map/ppermute | solution.py:221
  76.5 12.3 %collective-permute-start.28 = (f32[2,256,128]{2,1,0:T(8,128)S(1)}, f32[2,256,128]{2,1,0:T(8,128)S(1)}, u32[]{:S(2)}, u32[]{:S(2)}) collective-permute-start(f32[2,256,128]{2,1,0:T(8,128)S(1)} %get-tuple-element.84), channel_id=1, source_target_pairs={{0,25},{4,29},{2,27},{6,31},{1,0},{5,4},{3,2},{7,6},{8,1},{12,5},{... | collective-permute-start | bytes 786440 | tf_op jit(solution)/shard_map/ppermute | solution.py:221
  84.6 10.2 %collective-permute-start.12 = (f32[2,256,128]{2,1,0:T(8,128)S(1)}, f32[2,256,128]{2,1,0:T(8,128)S(1)}, u32[]{:S(2)}, u32[]{:S(2)}) collective-permute-start(f32[2,256,128]{2,1,0:T(8,128)S(1)} %get-tuple-element.64), channel_id=1, source_target_pairs={{0,25},{4,29},{2,27},{6,31},{1,0},{5,4},{3,2},{7,6},{8,1},{12,5},{... | collective-permute-start | bytes 786440 | tf_op jit(solution)/shard_map/ppermute | solution.py:221
  86.9 12.1 %collective-permute-start.23 = (f32[2,256,128]{2,1,0:T(8,128)S(1)}, f32[2,256,128]{2,1,0:T(8,128)S(1)}, u32[]{:S(2)}, u32[]{:S(2)}) collective-permute-start(f32[2,256,128]{2,1,0:T(8,128)S(1)} %get-tuple-element.77), channel_id=1, source_target_pairs={{0,0},{4,1},{2,2},{6,3},{1,4},{5,5},{3,6},{7,7},{8,8},{12,9},{10,1... | collective-permute-start | bytes 786440 | tf_op jit(solution)/shard_map/ppermute | solution.py:221
  91.0 21.1 %collective-permute-start.29 = (f32[2,256,128]{2,1,0:T(8,128)S(1)}, f32[2,256,128]{2,1,0:T(8,128)S(1)}, u32[]{:S(2)}, u32[]{:S(2)}) collective-permute-start(f32[2,256,128]{2,1,0:T(8,128)S(1)} %get-tuple-element.85), channel_id=1, source_target_pairs={{0,0},{4,1},{2,2},{6,3},{1,4},{5,5},{3,6},{7,7},{8,8},{12,9},{10,1... | collective-permute-start | bytes 786440 | tf_op jit(solution)/shard_map/ppermute | solution.py:221
  94.7 8.1 %collective-permute-start.24 = (f32[2,256,128]{2,1,0:T(8,128)S(1)}, f32[2,256,128]{2,1,0:T(8,128)S(1)}, u32[]{:S(2)}, u32[]{:S(2)}) collective-permute-start(f32[2,256,128]{2,1,0:T(8,128)S(1)} %get-tuple-element.78), channel_id=1, source_target_pairs={{0,4},{4,5},{2,6},{6,7},{1,8},{5,9},{3,10},{7,11},{8,12},{12,13},{... | collective-permute-start | bytes 786440 | tf_op jit(solution)/shard_map/ppermute | solution.py:221
  97.0 14.1 %collective-permute-start.17 = (f32[2,256,128]{2,1,0:T(8,128)S(1)}, f32[2,256,128]{2,1,0:T(8,128)S(1)}, u32[]{:S(2)}, u32[]{:S(2)}) collective-permute-start(f32[2,256,128]{2,1,0:T(8,128)S(1)} %get-tuple-element.69), channel_id=1, source_target_pairs={{0,0},{4,1},{2,2},{6,3},{1,4},{5,5},{3,6},{7,7},{8,8},{12,9},{10,1... | collective-permute-start | bytes 786440 | tf_op jit(solution)/shard_map/ppermute | solution.py:221
  98.9 12.2 %collective-permute-start.18 = (f32[2,256,128]{2,1,0:T(8,128)S(1)}, f32[2,256,128]{2,1,0:T(8,128)S(1)}, u32[]{:S(2)}, u32[]{:S(2)}) collective-permute-start(f32[2,256,128]{2,1,0:T(8,128)S(1)} %get-tuple-element.70), channel_id=1, source_target_pairs={{0,4},{4,5},{2,6},{6,7},{1,8},{5,9},{3,10},{7,11},{8,12},{12,13},{... | collective-permute-start | bytes 786440 | tf_op jit(solution)/shard_map/ppermute | solution.py:221
  99.0 13.1 %collective-permute-start.30 = (f32[2,256,128]{2,1,0:T(8,128)S(1)}, f32[2,256,128]{2,1,0:T(8,128)S(1)}, u32[]{:S(2)}, u32[]{:S(2)}) collective-permute-start(f32[2,256,128]{2,1,0:T(8,128)S(1)} %get-tuple-element.86), channel_id=1, source_target_pairs={{0,4},{4,5},{2,6},{6,7},{1,8},{5,9},{3,10},{7,11},{8,12},{12,13},{... | collective-permute-start | bytes 786440 | tf_op jit(solution)/shard_map/ppermute | solution.py:221
